TPU v7x, 32 devices: a whole 2x2x4 slice. The times are simulated.
32 devices in a mesh: row: 4 (over z), col: 4 (over y, x), layer: 2 (over core).
Axes of the slice: x: 2, y: 2, z: 4, core: 2. Of those that a mesh axis runs over, the one named last changes fastest.
Arguments:
- density: bfloat16 [2048, 2048], P('row', ('col', 'layer')), may hold values from -4 to 4
- block_mask: int32 [16, 16], P('row', ('col', 'layer')), may hold values from 0 to 1, as said below
- keep_mask: int32 [16, 16], P('row', ('col', 'layer')), may hold values 0 or 1
- branch_flag: int32 [16], P('row'), may hold values from 0 to 1
Outputs:
- updated: float32 [2048, 2048], P('row', ('col', 'layer'))
- trace_new: float32 [], replicated
Inputs may be any that keep to these rules, and one draw needn't show every extreme that they name: `block_mask`: symmetric, 1 on the diagonal; 1 where two blocks' centres in a periodic box lie within a cutoff distance of each other, else 0; block labels are in no spatial order. `keep_mask`: 0 or 1 for each block.
All inputs are finite; a program needn't handle non-finite values.
Results may differ from a plain program's by a relative error of at most 0.0004.
Values may be sent and summed in bfloat16 or wider, within the bound.
A program may use at most 64 MiB of HBM per device.

v0:
```python
import functools

import jax
import jax.numpy as jnp
from jax import lax
from jax.experimental import pallas as pl
from jax.experimental.pallas import tpu as pltpu
from jax.sharding import PartitionSpec as P

MESH = pl.DeviceIdType.MESH
CHUNKS = 4
HOP_CHUNKS = 1.8


def partner_of(index, step, size):
    if size & (size - 1):
        return (index + step) % size
    for bit in range(size.bit_length()):
        if step >> bit & 1:
            index = index + (1 - 2 * ((index // (1 << bit)) % 2)) * (1 << bit)
    return index


def passing_plan(n_row):
    plans, arrive = [], {}
    for row in range(n_row - 1):
        at_hand = dict(arrive)
        at_hand.update({(row, q): 0.0 for q in range(CHUNKS)})
        order, arrive, slot = [], {}, 0
        while at_hand:
            ready = [item for item, when in at_hand.items() if when <= slot]
            if ready:
                item = min(ready)
                order.append(item)
                arrive[item] = slot + 1 + HOP_CHUNKS
                del at_hand[item]
            slot += 1
        plans.append(order)
    return plans


def kernel(
    sizes, density_hbm, block_hbm, keep_hbm, flag_hbm, updated, trace,
    density, block_mask, keep_mask, branch_flag,
    row_panel, col_panel, trace_own, trace_in, local_sem,
    plane_send, plane_recv, side_send, right_send, left_send, z_recv,
    trace_send, trace_recv,
):
    n_row, n_col, n_layer = sizes
    rows, width = density.shape
    blk = rows // block_mask.shape[1]
    per = rows // width
    piece = rows // CHUNKS
    r, c, l = lax.axis_index("row"), lax.axis_index("col"), lax.axis_index("layer")
    me = c * n_layer + l
    has_left, has_right = r > 0, r < n_row - 1
    left, right = jnp.maximum(r - 1, 0), jnp.minimum(r + 1, n_row - 1)
    col_peers = [partner_of(c, d, n_col) for d in range(1, n_col)]
    layer_peers = [partner_of(l, d, n_layer) for d in range(1, n_layer)]

    loads = [
        pltpu.make_async_copy(source, target, local_sem.at[i])
        for i, (source, target) in enumerate([
            (block_hbm, block_mask), (density_hbm, density),
            (keep_hbm, keep_mask), (flag_hbm, branch_flag)])
    ]
    for load in loads:
        load.start()
    barrier = pltpu.get_barrier_semaphore()

    def greet(target):
        pl.semaphore_signal(barrier, inc=1, device_id=target, device_id_type=MESH)

    pl.when(has_left)(lambda: greet((left, c, l)))
    pl.when(has_right)(lambda: greet((right, c, l)))
    for peer in col_peers:
        for layer in range(n_layer):
            greet((r, peer, layer))
    for peer in layer_peers:
        greet((r, c, peer))
    for load in loads:
        load.wait()

    for i in range(rows // blk):
        for k in range(width // blk):
            at = (pl.ds(i * blk, blk), pl.ds(k * blk, blk))
            kept = jnp.full((blk, blk), block_mask[k, i].astype(jnp.float32))
            row_panel[(me,) + at] = density[at] * kept.astype(jnp.bfloat16)

    pl.semaphore_wait(
        barrier,
        jnp.where(has_left, 1, 0) + jnp.where(has_right, 1, 0) + n_col * n_layer - 1,
    )

    def span(q):
        return pl.ds(q * piece, piece)

    def z_copy(block, q, source, target, sems):
        return pltpu.make_async_remote_copy(
            src_ref=source, dst_ref=col_panel.at[block, span(q)],
            send_sem=sems.at[block, q], recv_sem=z_recv.at[block, q],
            device_id=(target, c, l), device_id_type=MESH,
        )

    def to_right(block, q, source):
        return z_copy(block, q, source, right, right_send)

    def to_left(block, q, source):
        return z_copy(block, q, source, left, left_send)

    def plane_copy(slot, peer, sems=None):
        return pltpu.make_async_remote_copy(
            src_ref=row_panel.at[slot], dst_ref=row_panel.at[slot],
            send_sem=plane_send.at[peer], recv_sem=plane_recv.at[slot],
            device_id=(r, peer, l), device_id_type=MESH,
        )

    def side_copy(slot, d):
        return pltpu.make_async_remote_copy(
            src_ref=row_panel.at[slot], dst_ref=row_panel.at[slot],
            send_sem=side_send.at[d, slot], recv_sem=plane_recv.at[slot],
            device_id=(r, c, layer_peers[d]), device_id_type=MESH,
        )

    plans = passing_plan(n_row)

    def pass_right(row, first, arrived):
        while first < len(plans[row]):
            block, q = plans[row][first]
            if block == row:
                to_right(row, q, row_panel.at[me, span(q)]).start()
            elif (block, q) in arrived:
                to_right(block, q, col_panel.at[block, span(q)]).start()
            else:
                break
            first += 1
        return first

    sent = [0] * (n_row - 1)
    for q in range(CHUNKS):
        pl.when(has_left)(lambda: to_left(r, q, row_panel.at[me, span(q)]).start())
    for row in range(n_row - 1):
        @pl.when(r == row)
        def _():
            sent[row] = pass_right(row, 0, ())
    for peer in col_peers:
        plane_copy(me, peer).start()
    for d in range(n_layer - 1):
        side_copy(me, d).start()

    def z_arrive(k, after_left=None, after_right=None):
        s, q = 1 + k // CHUNKS, k % CHUNKS

        @pl.when(r + s < n_row)
        def _():
            to_left(r + s, q, col_panel.at[r + s, span(q)]).wait_recv()
            pl.when(has_left)(
                lambda: to_left(r + s, q, col_panel.at[r + s, span(q)]).start())
            if after_right:
                after_right(r + s, q)

        for row in range(1, n_row):
            if k < len(plans[row - 1]):
                @pl.when(r == row)
                def _():
                    block, p = plans[row - 1][k]
                    to_right(block, p, col_panel.at[block, span(p)]).wait_recv()
                    if row < n_row - 1:
                        sent[row] = pass_right(row, sent[row], plans[row - 1][:k + 1])
                    if after_left:
                        after_left(row, k)

    def plane_arrive(peer):
        slot = peer * n_layer + l
        plane_copy(slot, peer).wait_recv()
        for d in range(n_layer - 1):
            side_copy(slot, d).start()

    def add_block(block):
        total = None
        for t in range(per):
            term = jnp.dot(
                row_panel[block * per + t], col_panel[block, pl.ds(t * width, width), :],
                preferred_element_type=jnp.float32)
            total = term if total is None else total + term
        updated[...] += total

    def add_chunk(block, q):
        start = q * piece
        updated[...] += jnp.dot(
            row_panel[block * per + start // width, :, pl.ds(start % width, piece)],
            col_panel[block, span(q), :], preferred_element_type=jnp.float32)

    on_diagonal = me // per == r
    corner = pl.multiple_of((me % per) * width, width)
    tiles = width // blk
    lanes = lax.broadcasted_iota(jnp.int32, (1, blk), 1)
    eye = (lax.broadcasted_iota(jnp.int32, (blk, blk), 0)
           == lax.broadcasted_iota(jnp.int32, (blk, blk), 1))

    def weight(t, if_square, otherwise):
        kept = keep_mask[t, (me % per) * tiles + t]
        chosen = jnp.where(branch_flag[(me % per) * tiles + t] == 1, if_square, otherwise)
        return (kept * chosen).astype(jnp.float32)

    def pair_sums(block, k):
        slot = block * per + k * blk // width
        out = []
        for t in range(tiles):
            ours = row_panel[slot, pl.ds(corner + t * blk, blk), pl.ds(k * blk % width, blk)]
            if block is r:
                theirs = row_panel[me, pl.ds(k * blk, blk), pl.ds(t * blk, blk)]
            else:
                theirs = col_panel[block, pl.ds(k * blk, blk), pl.ds(t * blk, blk)]
            product = jnp.dot(ours, theirs, preferred_element_type=jnp.float32)
            out.append(jnp.sum(jnp.where(eye, product, 0.0), axis=0, keepdims=True))
        return out

    def trace_copy(z, col, layer):
        return pltpu.make_async_remote_copy(
            src_ref=trace_own, dst_ref=trace_in.at[me],
            send_sem=trace_send.at[z, col, layer], recv_sem=trace_recv.at[me],
            device_id=(z, col, layer), device_id_type=MESH,
        )

    everyone = [(z, col, layer) for z in range(n_row) for col in range(n_col)
                for layer in range(n_layer)]

    def each_other(act):
        for z, col, layer in everyone:
            pl.when((z != r) | (col != c) | (layer != l))(
                functools.partial(act, z, col, layer))

    def add_trace(blocks, start):
        weights = [weight(t, 1, -1) for t in range(tiles)]
        part = spread = others = jnp.zeros((1, blk), jnp.float32)
        if not start:
            part, spread, others = (trace_own[n:n + 1, :] for n in range(3))
        for t in range(tiles if start else 0):
            own = row_panel[me, pl.ds(corner + t * blk, blk), pl.ds(t * blk, blk)]
            line = jnp.sum(
                jnp.where(eye, own.astype(jnp.float32), 0.0), axis=0, keepdims=True)
            part += weight(t, 0, 2) * line
            spread += jnp.where(lanes == me * tiles + t, weights[t], 0.0)
        for block in ([r] if start else []) + blocks:
            for k in range(rows // blk):
                lines = pair_sums(block, k)
                for t in range(tiles):
                    part += weights[t] * lines[t]
                if block is not r:
                    here = block * (rows // blk) + k
                    total = sum(jnp.sum(line, keepdims=True) for line in lines)
                    others += jnp.where(lanes == here, total, 0.0)
        trace_own[0:1, :] = part
        trace_own[1:2, :] = spread
        trace_own[2:3, :] = others

    def send_trace():
        trace_in[me] = trace_own[...]
        each_other(lambda z, col, layer: trace_copy(z, col, layer).start())

    last = n_row - 1
    for k in range(CHUNKS):
        z_arrive(k)
    near = [d for d in range(1, n_col) if d & (d - 1) == 0]
    far = [d for d in range(1, n_col) if d & (d - 1)]
    for d in near:
        plane_arrive(col_peers[d - 1])
    middle = (last - 1) * CHUNKS
    for k in range(CHUNKS, middle):
        z_arrive(k)
    for d in far:
        plane_arrive(col_peers[d - 1])
    for other in layer_peers:
        for d in range(n_col):
            slot = partner_of(c, d, n_col) * n_layer + other
            plane_copy(slot, c).wait_recv()

    early = [b for b, _ in plans[last - 1][:middle]].count(0) == CHUNKS
    for row in range(n_row):
        @pl.when(on_diagonal & (r == row))
        def _():
            pairs = [b for b in range(row + 1, n_row) if (row, b) != (0, last)]
            add_trace([0] if row == last and early else pairs, True)
            if 0 < row < last or row == last and early:
                send_trace()

    total = None
    for t in range(per):
        term = jnp.dot(
            row_panel[r * per + t], row_panel[me, pl.ds(t * width, width), :],
            preferred_element_type=jnp.float32)
        total = term if total is None else total + term
    updated[...] = total
    for s in range(1, last):
        pl.when((r - s >= 0) & has_right)(lambda: add_block(r - s))
        pl.when(r + s < n_row)(lambda: add_block(r + s))

    @pl.when(r == last)
    def _():
        for block, q in plans[last - 1][:middle]:
            add_chunk(block, q)

    def use_left(row, k):
        block, q = plans[last - 1][k]
        head = [b for b, _ in plans[last - 1][:k + 1]].count(0)
        if block == 0 and head == CHUNKS and not early:
            @pl.when(on_diagonal)
            def _():
                add_trace([0], False)
                send_trace()
        add_chunk(block, q)

    for k in range(middle, last * CHUNKS):
        z_arrive(k, use_left, add_chunk)
        if k == middle:
            pl.when(on_diagonal & (r == 0))(send_trace)

    for i in range(rows // blk):
        flag = jnp.full((blk, blk), branch_flag[i]) == 1
        for k in range(width // blk):
            at = (pl.ds(i * blk, blk), pl.ds(k * blk, blk))
            product = updated[at]
            doubled = 2.0 * row_panel[(me,) + at].astype(jnp.float32) - product
            kept = jnp.full((blk, blk), keep_mask[k, i].astype(jnp.float32))
            updated[at] = jnp.where(flag, product, doubled) * kept

    for q in range(CHUNKS):
        pl.when(has_left)(lambda: to_left(r, q, row_panel.at[me, span(q)]).wait_send())
        pl.when(has_right)(lambda: to_right(r, q, row_panel.at[me, span(q)]).wait_send())
        for s in range(1, n_row - 1):
            pl.when((r - s >= 0) & has_right)(
                lambda: to_right(r - s, q, col_panel.at[r - s, span(q)]).wait_send())
            pl.when((r + s < n_row) & has_left)(
                lambda: to_left(r + s, q, col_panel.at[r + s, span(q)]).wait_send())
    for peer in col_peers:
        plane_copy(me, peer).wait_send()
    for d in range(n_layer - 1):
        for col in range(n_col):
            side_copy(col * n_layer + l, d).wait_send()

    for slot in range(n_col * n_layer):
        @pl.when((slot // per != r) | (slot != me))
        def _():
            pltpu.make_async_remote_copy(
                src_ref=trace_own, dst_ref=trace_in.at[slot],
                send_sem=trace_send.at[0, 0, 0], recv_sem=trace_recv.at[slot],
                device_id=(r, c, l), device_id_type=MESH,
            ).wait_recv()
    parts = trace_in[0]
    for slot in range(1, n_col * n_layer):
        parts = parts + trace_in[slot]
    trace[0, 0] = jnp.sum(parts[0:1, :] + parts[1:2, :] * parts[2:3, :])
    pl.when(on_diagonal)(
        lambda: each_other(lambda z, col, layer: trace_copy(z, col, layer).wait_send()))


def on_device(sizes, density, block_mask, keep_mask, branch_flag):
    n_row, n_col, n_layer = sizes
    rows, width = density.shape
    blk = rows // block_mask.shape[0]
    dma = pltpu.SemaphoreType.DMA
    slots = n_col * n_layer
    vmem, smem = pl.BlockSpec(memory_space=pltpu.VMEM), pl.BlockSpec(memory_space=pltpu.SMEM)
    hbm = pl.BlockSpec(memory_space=pltpu.HBM)
    panel_bytes = 2 * rows * width * (slots + n_row + 1)
    updated, trace = pl.pallas_call(
        functools.partial(kernel, sizes),
        out_shape=(
            jax.ShapeDtypeStruct((rows, width), jnp.float32),
            jax.ShapeDtypeStruct((1, 1), jnp.float32),
        ),
        in_specs=[hbm, hbm, hbm, hbm],
        out_specs=(vmem, smem),
        scratch_shapes=[
            pltpu.VMEM((rows, width), jnp.bfloat16),
            pltpu.SMEM(block_mask.T.shape, jnp.int32),
            pltpu.SMEM(keep_mask.T.shape, jnp.int32),
            pltpu.SMEM(branch_flag.shape, jnp.int32),
            pltpu.VMEM((slots, rows, width), jnp.bfloat16),
            pltpu.VMEM((n_row, rows, width), jnp.bfloat16),
            pltpu.VMEM((3, blk), jnp.float32),
            pltpu.VMEM((slots, 3, blk), jnp.float32),
            dma((4,)),
            dma((n_col,)),
            dma((slots,)),
            dma((max(n_layer - 1, 1), slots)),
            dma((n_row, CHUNKS)),
            dma((n_row, CHUNKS)),
            dma((n_row, CHUNKS)),
            dma((n_row, n_col, n_layer)),
            dma((slots,)),
        ],
        compiler_params=pltpu.CompilerParams(
            collective_id=0, has_side_effects=True,
            vmem_limit_bytes=panel_bytes + 8 * rows * width + (2 << 20)),
    )(*[
        pltpu.with_memory_space_constraint(x, pltpu.HBM)
        for x in (density, block_mask.T, keep_mask.T, branch_flag)
    ])
    return updated, trace[0, 0]


def solution(mesh):
    sizes = tuple(mesh.shape[name] for name in ("row", "col", "layer"))
    in_specs = (
        P("row", ("col", "layer")),
        P("row", ("col", "layer")),
        P("row", ("col", "layer")),
        P("row"),
    )
    out_specs = (P("row", ("col", "layer")), P())
    return jax.shard_map(
        functools.partial(on_device, sizes), mesh=mesh, in_specs=in_specs,
        out_specs=out_specs, check_vma=False,
    )
```

profile of v0, /device:TPU:0, one launch (start us, length us, event | category | flops | bytes accessed | tf_op | source)
XLA Modules:
  0.0 31.4 jit_solution(15019999121851392682)
XLA Ops:
  0.6 28.3 %shard_map.59 = (f32[512,256]{1,0:T(8,128)S(1)}, f32[1,1]{1,0:T(1,128)}) custom-call(bf16[512,256]{1,0:T(8,128)(2,1)} %density_hbm.1, s32[2,4]{1,0:T(2,128)} %bitcast.3, s32[2,4]{1,0:T(2,128)} %bitcast.4, s32[4]{0:T(128)} %flag_hbm.1), custom_call_target="tpu_custom_call" | custom-call | tf_op jit(solution)/shard_map/pallas_call | solution.py:367
  28.9 0.8 %copy.8 = f32[512,256]{1,0:T(8,128)} copy(f32[512,256]{1,0:T(8,128)S(1)} %get-tuple-element.8) | data formatting | bytes 1048576
where the time goes:
time: 31.6 us; the launch traced here: 31.4 us
  Pallas kernels  28.3 us (90%)
  between operations  2.33 us (7%)
  local copies, waits for them, and re-layouts  0.8 us (3%)
    pallas_call x1, Pallas kernels, on_device(): pl.pallas_call(functools.partial(kernel, sizes), out_shape=(jax.ShapeDtyp...  28.3 us
    unnamed x1, local copies, waits for them, and re-layouts  0.8 us

commit v1 on v0

v1 whole, which is shorter than its diff:
```python
import functools

import jax
import jax.numpy as jnp
from jax import lax
from jax.experimental import pallas as pl
from jax.experimental.pallas import tpu as pltpu
from jax.sharding import PartitionSpec as P

MESH = pl.DeviceIdType.MESH
CHUNKS = 4
AHEAD = 2


def partner_of(index, step, size):
    if size & (size - 1):
        return (index + step) % size
    for bit in range(size.bit_length()):
        if step >> bit & 1:
            index = index + (1 - 2 * ((index // (1 << bit)) % 2)) * (1 << bit)
    return index


def passing_plan(n_row, late):
    plans = []
    for row in range(n_row - 1):
        order = [(block, q) for block in range(row, -1, -1) for q in range(CHUNKS)]
        for q in range(CHUNKS - late[min(row, len(late) - 1)], CHUNKS):
            if row:
                order.remove((1, q))
                order.append((1, q))
        plans.append(order)
    return plans


def kernel(
    sizes, density_hbm, block_hbm, keep_hbm, flag_hbm, updated, lines,
    density, block_mask, keep_mask, branch_flag,
    row_panel, col_panel, trace_own, trace_in, local_sem,
    plane_send, plane_recv, side_send, right_send, left_send, z_recv,
    trace_send, trace_recv, trace_sum, sum_send, sum_recv, ready,
):
    n_row, n_col, n_layer = sizes
    rows, width = density.shape
    blk = rows // block_mask.shape[1]
    per = rows // width
    piece = rows // CHUNKS
    slots = n_col * n_layer
    last = n_row - 1
    r, c, l = lax.axis_index("row"), lax.axis_index("col"), lax.axis_index("layer")
    me = c * n_layer + l
    has_left, has_right = r > 0, r < last
    left, right = jnp.maximum(r - 1, 0), jnp.minimum(r + 1, last)
    col_peers = [partner_of(c, d, n_col) for d in range(1, n_col)]
    layer_peers = [partner_of(l, d, n_layer) for d in range(1, n_layer)]
    plane_peers = [(p, q) for p in col_peers for q in range(n_layer)]
    plane_peers += [(c, q) for q in layer_peers]

    loads = [
        pltpu.make_async_copy(source, target, local_sem.at[i])
        for i, (source, target) in enumerate([
            (block_hbm, block_mask), (density_hbm, density),
            (keep_hbm, keep_mask), (flag_hbm, branch_flag)])
    ]
    for load in loads:
        load.start()

    barrier = pltpu.get_barrier_semaphore()

    def greet(target):
        pl.semaphore_signal(barrier, inc=1, device_id=target, device_id_type=MESH)

    def answer(which, target):
        pl.semaphore_signal(
            ready.at[which], inc=1, device_id=target, device_id_type=MESH)

    pl.when(has_right)(lambda: greet((right, c, l)))
    for p, q in plane_peers:
        pl.when(p * n_layer + q > me)(functools.partial(greet, (r, p, q)))
    below, above = jnp.where(has_left, 1, 0) + me, slots - 1 - me
    pl.when(below > 0)(lambda: pl.semaphore_wait(barrier, below))
    pl.when(has_left)(lambda: answer(0, (left, c, l)))
    for p, q in plane_peers:
        pl.when(p * n_layer + q < me)(functools.partial(answer, 1, (r, p, q)))
    for load in loads:
        load.wait()

    for i in range(rows // blk):
        for k in range(width // blk):
            at = (pl.ds(i * blk, blk), pl.ds(k * blk, blk))
            kept = jnp.full((blk, blk), block_mask[k, i].astype(jnp.float32))
            row_panel[(me,) + at] = density[at] * kept.astype(jnp.bfloat16)

    def span(q):
        return pl.ds(q * piece, piece)

    def z_copy(block, q, source, target, sem):
        return pltpu.make_async_remote_copy(
            src_ref=source, dst_ref=col_panel.at[block, span(q)],
            send_sem=sem.at[0], recv_sem=z_recv.at[block, q],
            device_id=(target, c, l), device_id_type=MESH,
        )

    def to_right(block, q, source):
        return z_copy(block, q, source, right, right_send)

    def to_left(block, q, source):
        return z_copy(block, q, source, left, left_send)

    def half_copy(slot, h, sem, target):
        half = pl.ds(h * (rows // 2), rows // 2)
        return pltpu.make_async_remote_copy(
            src_ref=row_panel.at[slot, half], dst_ref=row_panel.at[slot, half],
            send_sem=sem.at[0], recv_sem=plane_recv.at[slot, h],
            device_id=target, device_id_type=MESH,
        )

    def plane_copy(slot, h, peer):
        return half_copy(slot, h, plane_send, (r, peer, l))

    def side_copies(slot, h):
        for other in layer_peers:
            half_copy(slot, h, side_send, (r, c, other)).start()

    def side_wait(slot):
        for h in range(2):
            half_copy(slot, h, side_send, (r, c, l)).wait_recv()

    bits = [d for d in range(1, n_col) if d & (d - 1) == 0]
    relayed = [lo | hi for hi in bits for lo in bits if lo < hi]
    if n_col & (n_col - 1):
        bits, relayed = list(range(1, n_col)), []
    direct = [d for d in range(1, n_col) if d not in relayed]
    halves = {d: (1, 0) if relayed and d > 1 else (0, 1) for d in range(1, n_col)}

    def plane_start(chosen):
        for turn in range(2):
            for d in direct:
                peer = col_peers[d - 1]
                pl.when(chosen(peer))(
                    lambda: plane_copy(me, halves[d][turn], peer).start())

    def plane_arrive(d, turn):
        peer, h = col_peers[d - 1], halves[d][turn]
        slot = peer * n_layer + l
        plane_copy(slot, h, peer).wait_recv()
        for other in bits if relayed and d in bits else []:
            if (other > d) == (h == 0) and other != d:
                plane_copy(slot, h, col_peers[other - 1]).start()
        side_copies(slot, h)

    rightward = passing_plan(n_row, (0, 3)) + [[]]
    leftward = [[]] + [[(last - b, q) for b, q in plan]
                       for plan in reversed(passing_plan(n_row, (0, 1, 2)))]
    from_left = [[]] + rightward[:-1]
    from_right = leftward[1:] + [[]]

    def pass_on(copy, row, plan, first, arrived, limit=None):
        while first < len(plan) and (limit is None or first < limit):
            block, q = plan[first]
            if block == row:
                copy(row, q, row_panel.at[me, span(q)]).start()
            elif (block, q) in arrived:
                copy(block, q, col_panel.at[block, span(q)]).start()
            else:
                break
            first += 1
        return first

    sent_left, sent_right = [0] * n_row, [0] * n_row
    for row in range(1, n_row):
        @pl.when(r == row)
        def _():
            sent_left[row] = pass_on(to_left, row, leftward[row], 0, (), AHEAD)
    plane_start(lambda peer: peer < c)
    pl.when(has_right)(lambda: pl.semaphore_wait(ready.at[0], 1))
    for row in range(last):
        @pl.when(r == row)
        def _():
            sent_right[row] = pass_on(to_right, row, rightward[row], 0, (), AHEAD)
    pl.when(above > 0)(lambda: pl.semaphore_wait(ready.at[1], above))
    for row in range(n_row):
        @pl.when(r == row)
        def _():
            sent_left[row] = pass_on(to_left, row, leftward[row], sent_left[row], ())
            sent_right[row] = pass_on(to_right, row, rightward[row], sent_right[row], ())
    plane_start(lambda peer: peer > c)
    for h in range(2):
        side_copies(me, h)

    def z_arrive(k, then=None):
        for row in range(n_row):
            if k < max(len(from_right[row]), len(from_left[row])):
                @pl.when(r == row)
                def _():
                    if k < len(from_left[row]):
                        block, q = from_left[row][k]
                        to_right(block, q, col_panel.at[block, span(q)]).wait_recv()
                        sent_right[row] = pass_on(
                            to_right, row, rightward[row], sent_right[row],
                            from_left[row][:k + 1])
                        if then:
                            then(row, from_left[row], k)
                    if k < len(from_right[row]):
                        block, q = from_right[row][k]
                        to_left(block, q, col_panel.at[block, span(q)]).wait_recv()
                        sent_left[row] = pass_on(
                            to_left, row, leftward[row], sent_left[row],
                            from_right[row][:k + 1])
                        if then:
                            then(row, from_right[row], k)

    def terms(block, start, size):
        out = []
        while size:
            step = min(size, width - start % width)
            out.append(jnp.dot(
                row_panel[block * per + start // width, :, pl.ds(start % width, step)],
                col_panel[block, pl.ds(start, step), :],
                preferred_element_type=jnp.float32))
            start, size = start + step, size - step
        return out

    def add(products):
        total = products[0]
        for product in products[1:]:
            total = total + product
        updated[...] += total

    on_diagonal = me // per == r
    corner = pl.multiple_of((me % per) * width, width)
    tiles = width // blk
    lanes = lax.broadcasted_iota(jnp.int32, (1, blk), 1)
    eye = (lax.broadcasted_iota(jnp.int32, (blk, blk), 0)
           == lax.broadcasted_iota(jnp.int32, (blk, blk), 1))

    def weight(t, if_square, otherwise):
        kept = keep_mask[t, (me % per) * tiles + t]
        chosen = jnp.where(branch_flag[(me % per) * tiles + t] == 1, if_square, otherwise)
        return (kept * chosen).astype(jnp.float32)

    def pair_sums(block, k):
        slot = block * per + k * blk // width
        out = []
        for t in range(tiles):
            ours = row_panel[slot, pl.ds(corner + t * blk, blk), pl.ds(k * blk % width, blk)]
            if block is r:
                theirs = row_panel[me, pl.ds(k * blk, blk), pl.ds(t * blk, blk)]
            else:
                theirs = col_panel[block, pl.ds(k * blk, blk), pl.ds(t * blk, blk)]
            product = jnp.dot(ours, theirs, preferred_element_type=jnp.float32)
            out.append(jnp.sum(jnp.where(eye, product, 0.0), axis=0, keepdims=True))
        return out

    def trace_copy(z, col, layer):
        return pltpu.make_async_remote_copy(
            src_ref=trace_own, dst_ref=trace_in.at[me],
            send_sem=trace_send.at[0], recv_sem=trace_recv.at[jnp.where(r > 0, 1, 0)],
            device_id=(z, col, layer), device_id_type=MESH,
        )

    def heirs(row):
        planes = range(n_row) if row == 0 else range(1, max(row + 1, last))
        return [(z, col, layer) for z in planes for col in range(n_col)
                for layer in range(n_layer)]

    def add_trace(blocks, start):
        weights = [weight(t, 1, -1) for t in range(tiles)]
        part = spread = others = jnp.zeros((1, blk), jnp.float32)
        if not start:
            part, spread, others = (trace_own[n:n + 1, :] for n in range(3))
        for t in range(tiles if start else 0):
            own = row_panel[me, pl.ds(corner + t * blk, blk), pl.ds(t * blk, blk)]
            line = jnp.sum(
                jnp.where(eye, own.astype(jnp.float32), 0.0), axis=0, keepdims=True)
            part += weight(t, 0, 2) * line
            spread += jnp.where(lanes == me * tiles + t, weights[t], 0.0)
        for block in ([r] if start else []) + blocks:
            for k in range(rows // blk):
                sums = pair_sums(block, k)
                for t in range(tiles):
                    part += weights[t] * sums[t]
                if block is not r:
                    here = block * (rows // blk) + k
                    total = sum(jnp.sum(line, keepdims=True) for line in sums)
                    others += jnp.where(lanes == here, total, 0.0)
        trace_own[0:1, :] = part
        trace_own[1:2, :] = spread
        trace_own[2:3, :] = others

    def send_trace(row):
        trace_in[me] = trace_own[...]
        for z, col, layer in heirs(row):
            pl.when((z != row) | (col != c) | (layer != l))(
                lambda: trace_copy(z, col, layer).start())

    middle = (last - 1) * CHUNKS
    early = [b for b, _ in from_right[0][:middle]].count(last) == CHUNKS

    def partner(b, row):
        return (b * per // n_layer) ^ (row * per // n_layer)

    def diagonal(row):
        @pl.when(on_diagonal & (r == row))
        def _():
            pairs = [0] + list(range(row + 1, n_row)) if row else [last] if early else []
            add_trace([] if row == last else pairs, True)
            if row > 0 or early:
                send_trace(row)

    pl.when(has_left)(lambda: pl.semaphore_wait(ready.at[2], 1))
    pl.when(has_right)(lambda: answer(2, (right, c, l)))
    for other in layer_peers:
        side_wait(c * n_layer + other)
    diagonal(last)
    for k in range(CHUNKS // 2):
        z_arrive(k)
    for d in direct:
        plane_arrive(d, 0)
    for k in range(CHUNKS // 2, CHUNKS):
        z_arrive(k)
    for d in direct:
        plane_arrive(d, 1)
    soon = CHUNKS + 1
    for k in range(CHUNKS, soon):
        z_arrive(k)
    for other in layer_peers:
        for d in direct:
            side_wait(col_peers[d - 1] * n_layer + other)
    def needs(row):
        blocks = {0: [last], last: []}.get(row, [0] + list(range(row + 1, n_row)))
        late = [b for b in blocks if partner(b, row) in relayed]
        for b in blocks:
            arrived = (from_left if b < row else from_right)[row][:soon]
            late += [b] if [x for x, _ in arrived].count(b) < CHUNKS else []
        return late

    quick = [row for row in range(1, last) if not needs(row)]
    for row in quick:
        diagonal(row)
    for turn in range(2):
        for d in relayed:
            plane_arrive(d, turn)
    for k in range(soon, middle):
        z_arrive(k)
    for other in layer_peers:
        for d in relayed:
            side_wait(col_peers[d - 1] * n_layer + other)
    for row in range(last):
        if row not in quick:
            diagonal(row)

    total = None
    for t in range(per):
        term = jnp.dot(
            row_panel[r * per + t], row_panel[me, pl.ds(t * width, width), :],
            preferred_element_type=jnp.float32)
        total = term if total is None else total + term
    updated[...] = total
    inner = has_left & has_right
    for s in range(1, last):
        pl.when((r - s >= 0) & inner)(lambda: add(terms(r - s, 0, rows)))
        pl.when((r + s <= last) & inner)(lambda: add(terms(r + s, 0, rows)))
    for row, arrived in ((0, from_right[0]), (last, from_left[last])):
        @pl.when(r == row)
        def _():
            products = []
            for block in range(n_row):
                held = sorted(q for b, q in arrived[:middle] if b == block)
                if held:
                    assert held == list(range(len(held)))
                    products += terms(block, 0, len(held) * piece)
            add(products)

    def finish(row, arrived, k):
        block, q = arrived[k]
        held = [b for b, _ in arrived[:k + 1]].count(last)
        if row == 0 and block == last and held == CHUNKS and not early:
            @pl.when(on_diagonal)
            def _():
                add_trace([last], False)
                send_trace(0)
        add(terms(block, q * piece, piece))

    for k in range(middle, last * CHUNKS):
        z_arrive(k, finish)

    for i in range(rows // blk):
        flag = jnp.full((blk, blk), branch_flag[i]) == 1
        for k in range(width // blk):
            at = (pl.ds(i * blk, blk), pl.ds(k * blk, blk))
            product = updated[at]
            doubled = 2.0 * row_panel[(me,) + at].astype(jnp.float32) - product
            kept = jnp.full((blk, blk), keep_mask[k, i].astype(jnp.float32))
            updated[at] = jnp.where(flag, product, doubled) * kept

    def heard(first, count, sem):
        pltpu.make_async_remote_copy(
            src_ref=trace_in.at[pl.ds(first, count)],
            dst_ref=trace_in.at[pl.ds(first, count)],
            send_sem=trace_send.at[0], recv_sem=trace_recv.at[sem],
            device_id=(r, c, l), device_id_type=MESH,
        ).wait_recv()

    def hear(first, count, sem):
        pl.when(on_diagonal & (me >= first) & (me < first + count))(
            lambda: heard(first, count - 1, sem))
        pl.when(jnp.logical_not(on_diagonal & (me >= first) & (me < first + count)))(
            lambda: heard(first, count, sem))

    def sum_of(first, count):
        total = trace_in[first]
        for slot in range(first + 1, first + count):
            total = total + trace_in[slot]
        return total

    def sum_copy(n, target):
        return pltpu.make_async_remote_copy(
            src_ref=trace_sum.at[n], dst_ref=trace_sum.at[0],
            send_sem=sum_send.at[n], recv_sem=sum_recv.at[0],
            device_id=(target, c, l), device_id_type=MESH,
        )

    @pl.when(inner)
    def _():
        hear(per, slots - per, 1)

    @pl.when(r == 1)
    def _():
        trace_sum[1] = sum_of(per, slots - per)
        sum_copy(1, 0).start()

    @pl.when(r == last - 1)
    def _():
        trace_sum[2] = sum_of(per, slots - 2 * per)
        sum_copy(2, last).start()

    for row in range(n_row):
        @pl.when(r == row)
        def _():
            for copy, plan, sem in (
                    (to_left, leftward[row], left_send),
                    (to_right, rightward[row], right_send)):
                if plan:
                    blocks = pl.ds(0, len(plan) // CHUNKS)
                    pltpu.make_async_remote_copy(
                        src_ref=col_panel.at[blocks], dst_ref=col_panel.at[blocks],
                        send_sem=sem.at[0], recv_sem=z_recv.at[0, 0],
                        device_id=(left, c, l), device_id_type=MESH,
                    ).wait_send()

    def sent_slots(count, ref, sem):
        pltpu.make_async_remote_copy(
            src_ref=ref.at[pl.ds(0, count)], dst_ref=ref.at[pl.ds(0, count)],
            send_sem=sem.at[0], recv_sem=plane_recv.at[0, 0],
            device_id=(r, c, l), device_id_type=MESH,
        ).wait_send()

    sent_slots(n_col - 1, row_panel, plane_send)
    sent_slots((n_layer - 1) * n_col, row_panel, side_send)

    hear(0, per, 0)

    @pl.when(r == last)
    def _():
        hear(last * per, per, 1)

    @pl.when(jnp.logical_not(inner))
    def _():
        sum_copy(1, 0).wait_recv()

    @pl.when(inner)
    def _():
        lines[...] = sum_of(0, slots)

    @pl.when(r == 0)
    def _():
        lines[...] = sum_of(0, per) + trace_sum[0]

    @pl.when(r == last)
    def _():
        lines[...] = sum_of(0, per) + sum_of(last * per, per) + trace_sum[0]

    pl.when(r == 1)(lambda: sum_copy(1, 0).wait_send())
    pl.when(r == last - 1)(lambda: sum_copy(2, last).wait_send())
    for row in range(n_row):
        pl.when(on_diagonal & (r == row))(
            lambda: sent_slots(len(heirs(row)) - 1, trace_in, trace_send))


def deliver(updated, lines, out, trace):
    out[...] = updated[...]
    trace[0, 0] = jnp.sum(lines[0:1, :] + lines[1:2, :] * lines[2:3, :])


def on_device(sizes, density, block_mask, keep_mask, branch_flag):
    n_row, n_col, n_layer = sizes
    rows, width = density.shape
    blk = rows // block_mask.shape[0]
    dma = pltpu.SemaphoreType.DMA
    slots = n_col * n_layer
    vmem, smem = pl.BlockSpec(memory_space=pltpu.VMEM), pl.BlockSpec(memory_space=pltpu.SMEM)
    hbm = pl.BlockSpec(memory_space=pltpu.HBM)
    panel_bytes = 2 * rows * width * (slots + n_row + 1)
    updated, lines = pl.pallas_call(
        functools.partial(kernel, sizes),
        out_shape=(
            jax.ShapeDtypeStruct((rows, width), jnp.float32),
            jax.ShapeDtypeStruct((3, blk), jnp.float32),
        ),
        in_specs=[hbm, hbm, hbm, hbm],
        out_specs=(vmem, vmem),
        scratch_shapes=[
            pltpu.VMEM((rows, width), jnp.bfloat16),
            pltpu.SMEM(block_mask.T.shape, jnp.int32),
            pltpu.SMEM(keep_mask.T.shape, jnp.int32),
            pltpu.SMEM(branch_flag.shape, jnp.int32),
            pltpu.VMEM((slots, rows, width), jnp.bfloat16),
            pltpu.VMEM((n_row, rows, width), jnp.bfloat16),
            pltpu.VMEM((3, blk), jnp.float32),
            pltpu.VMEM((n_row * slots, 3, blk), jnp.float32),
            dma((4,)),
            dma((1,)),
            dma((slots, 2)),
            dma((1,)),
            dma((1,)),
            dma((1,)),
            dma((n_row, CHUNKS)),
            dma((1,)),
            dma((2,)),
            pltpu.VMEM((3, 3, blk), jnp.float32),
            dma((3,)),
            dma((1,)),
            pltpu.SemaphoreType.REGULAR((3,)),
        ],
        compiler_params=pltpu.CompilerParams(
            collective_id=0, has_side_effects=True,
            vmem_limit_bytes=panel_bytes + 8 * rows * width + (4 << 20)),
    )(*[
        pltpu.with_memory_space_constraint(x, pltpu.HBM)
        for x in (density, block_mask.T, keep_mask.T, branch_flag)
    ])
    updated, trace = pl.pallas_call(
        deliver,
        out_shape=(
            jax.ShapeDtypeStruct((rows, width), jnp.float32),
            jax.ShapeDtypeStruct((1, 1), jnp.float32),
        ),
        in_specs=[vmem, vmem],
        out_specs=(vmem, smem),
        compiler_params=pltpu.CompilerParams(
            vmem_limit_bytes=8 * rows * width + (4 << 20)),
    )(updated, lines)
    return updated, trace[0, 0]


def solution(mesh):
    sizes = tuple(mesh.shape[name] for name in ("row", "col", "layer"))
    in_specs = (
        P("row", ("col", "layer")),
        P("row", ("col", "layer")),
        P("row", ("col", "layer")),
        P("row"),
    )
    out_specs = (P("row", ("col", "layer")), P())
    return jax.shard_map(
        functools.partial(on_device, sizes), mesh=mesh, in_specs=in_specs,
        out_specs=out_specs, check_vma=False,
    )
```

time: 31.6 us -> 26.5 us (0.84)
  Pallas kernels: 28.3 us -> 25.7 us
  between operations: 2.33 us -> 0.64 us
  local copies, waits for them, and re-layouts: 0.8 us -> 0 us
    pallas_call x1, Pallas kernels: 28.3 us -> 24.8 us  [on_device(): pl.pallas_call(functools.partial(kernel, sizes), out_shape=(jax.ShapeDtyp...]
    pallas_call x0 -> x1, Pallas kernels: none -> 0.84 us  [on_device(): pl.pallas_call(deliver, out_shape=(jax.ShapeDtypeStruct((rows, width), jn...]
    unnamed x1 -> x0, local copies, waits for them, and re-layouts: 0.8 us -> none
where the time goes in v1:
time: 26.5 us; the launch traced here: 26.3 us
  Pallas kernels  25.7 us (97%)
  between operations  0.64 us (2%)
    pallas_call x1, Pallas kernels, on_device(): pl.pallas_call(functools.partial(kernel, sizes), out_shape=(jax.ShapeDtyp...  24.8 us
    pallas_call x1, Pallas kernels, on_device(): pl.pallas_call(deliver, out_shape=(jax.ShapeDtypeStruct((rows, width), jn...  0.84 us

profile of v1, /device:TPU:0, one launch (start us, length us, event | category | flops | bytes accessed | tf_op | source)
XLA Modules:
  0.0 26.3 jit_solution(8263328241748047198)
XLA Ops:
  0.6 24.8 %shard_map.59 = (f32[512,256]{1,0:T(8,128)S(1)}, f32[3,128]{1,0:T(4,128)S(1)}) custom-call(bf16[512,256]{1,0:T(8,128)(2,1)} %density_hbm.1, s32[2,4]{1,0:T(2,128)} %bitcast.3, s32[2,4]{1,0:T(2,128)} %bitcast.4, s32[4]{0:T(128)} %flag_hbm.1), custom_call_target="tpu_custom_call" | custom-call | tf_op jit(solution)/shard_map/pallas_call | solution.py:505
  25.5 0.8 %shard_map.60 = (f32[512,256]{1,0:T(8,128)}, f32[1,1]{1,0:T(1,128)}) custom-call(f32[512,256]{1,0:T(8,128)S(1)} %get-tuple-element.6.updated, f32[3,128]{1,0:T(4,128)S(1)} %get-tuple-element.7.lines), custom_call_target="tpu_custom_call" | custom-call | tf_op jit(solution)/shard_map/pallas_call | solution.py:543

commit v2 on v1

--- a/solution.py
+++ b/solution.py
@@ -21,16 +21,13 @@
     return index
 
 
-def passing_plan(n_row, late):
-    plans = []
-    for row in range(n_row - 1):
-        order = [(block, q) for block in range(row, -1, -1) for q in range(CHUNKS)]
-        for q in range(CHUNKS - late[min(row, len(late) - 1)], CHUNKS):
-            if row:
-                order.remove((1, q))
-                order.append((1, q))
-        plans.append(order)
-    return plans
+def passing_plans(n_row):
+    last = n_row - 1
+    blocks = [[(b, q) for q in range(CHUNKS)] for b in range(n_row)]
+    rightward = [sum(blocks[row::-1], []) for row in range(last)] + [[]]
+    leftward = [[]] + [sum(blocks[row:], []) for row in range(1, n_row)]
+    leftward[1].append(leftward[1].pop(CHUNKS - 1))
+    return rightward, leftward
 
 
 def kernel(
@@ -38,7 +35,7 @@
     density, block_mask, keep_mask, branch_flag,
     row_panel, col_panel, trace_own, trace_in, local_sem,
     plane_send, plane_recv, side_send, right_send, left_send, z_recv,
-    trace_send, trace_recv, trace_sum, sum_send, sum_recv, ready,
+    trace_send, trace_recv, ready,
 ):
     n_row, n_col, n_layer = sizes
     rows, width = density.shape
@@ -149,25 +146,31 @@
                 plane_copy(slot, h, col_peers[other - 1]).start()
         side_copies(slot, h)
 
-    rightward = passing_plan(n_row, (0, 3)) + [[]]
-    leftward = [[]] + [[(last - b, q) for b, q in plan]
-                       for plan in reversed(passing_plan(n_row, (0, 1, 2)))]
+    rightward, leftward = passing_plans(n_row)
     from_left = [[]] + rightward[:-1]
     from_right = leftward[1:] + [[]]
 
-    def pass_on(copy, row, plan, first, arrived, limit=None):
-        while first < len(plan) and (limit is None or first < limit):
+    on_diagonal = me // per == r
+
+    def pass_on(copy, row, plan, first, arrived, stop=None, hold=None):
+        while first < len(plan) and (stop is None or first < stop):
             block, q = plan[first]
             if block == row:
-                copy(row, q, row_panel.at[me, span(q)]).start()
+                source = row_panel.at[me, span(q)]
             elif (block, q) in arrived:
-                copy(block, q, col_panel.at[block, span(q)]).start()
+                source = col_panel.at[block, span(q)]
             else:
                 break
+            if hold is None or first < hold:
+                copy(block, q, source).start()
+            else:
+                pl.when(jnp.logical_not(on_diagonal))(
+                    functools.partial(lambda f: f.start(), copy(block, q, source)))
             first += 1
         return first
 
     sent_left, sent_right = [0] * n_row, [0] * n_row
+    hold_left, hold_right = {1: last * CHUNKS - 3}, {last - 1: 2 * CHUNKS - 1}
     for row in range(1, n_row):
         @pl.when(r == row)
         def _():
@@ -182,8 +185,10 @@
     for row in range(n_row):
         @pl.when(r == row)
         def _():
-            sent_left[row] = pass_on(to_left, row, leftward[row], sent_left[row], ())
-            sent_right[row] = pass_on(to_right, row, rightward[row], sent_right[row], ())
+            sent_left[row] = pass_on(
+                to_left, row, leftward[row], sent_left[row], (), None, hold_left.get(row))
+            sent_right[row] = pass_on(
+                to_right, row, rightward[row], sent_right[row], (), None, hold_right.get(row))
     plane_start(lambda peer: peer > c)
     for h in range(2):
         side_copies(me, h)
@@ -193,22 +198,22 @@
             if k < max(len(from_right[row]), len(from_left[row])):
                 @pl.when(r == row)
                 def _():
+                    if k < len(from_right[row]):
+                        block, q = from_right[row][k]
+                        to_left(block, q, col_panel.at[block, span(q)]).wait_recv()
+                        sent_left[row] = pass_on(
+                            to_left, row, leftward[row], sent_left[row],
+                            from_right[row][:k + 1], None, hold_left.get(row))
+                        if then:
+                            then(row, from_right[row], k)
                     if k < len(from_left[row]):
                         block, q = from_left[row][k]
                         to_right(block, q, col_panel.at[block, span(q)]).wait_recv()
                         sent_right[row] = pass_on(
                             to_right, row, rightward[row], sent_right[row],
-                            from_left[row][:k + 1])
+                            from_left[row][:k + 1], None, hold_right.get(row))
                         if then:
                             then(row, from_left[row], k)
-                    if k < len(from_right[row]):
-                        block, q = from_right[row][k]
-                        to_left(block, q, col_panel.at[block, span(q)]).wait_recv()
-                        sent_left[row] = pass_on(
-                            to_left, row, leftward[row], sent_left[row],
-                            from_right[row][:k + 1])
-                        if then:
-                            then(row, from_right[row], k)
 
     def terms(block, start, size):
         out = []
@@ -227,7 +232,6 @@
             total = total + product
         updated[...] += total
 
-    on_diagonal = me // per == r
     corner = pl.multiple_of((me % per) * width, width)
     tiles = width // blk
     lanes = lax.broadcasted_iota(jnp.int32, (1, blk), 1)
@@ -255,13 +259,11 @@
     def trace_copy(z, col, layer):
         return pltpu.make_async_remote_copy(
             src_ref=trace_own, dst_ref=trace_in.at[me],
-            send_sem=trace_send.at[0], recv_sem=trace_recv.at[jnp.where(r > 0, 1, 0)],
+            send_sem=trace_send.at[0], recv_sem=trace_recv.at[0],
             device_id=(z, col, layer), device_id_type=MESH,
         )
 
-    def heirs(row):
-        planes = range(n_row) if row == 0 else range(1, max(row + 1, last))
-        return [(z, col, layer) for z in planes for col in range(n_col)
+    everyone = [(z, col, layer) for z in range(n_row) for col in range(n_col)
                 for layer in range(n_layer)]
 
     def add_trace(blocks, start):
@@ -290,29 +292,48 @@
 
     def send_trace(row):
         trace_in[me] = trace_own[...]
-        for z, col, layer in heirs(row):
+        for z, col, layer in everyone:
             pl.when((z != row) | (col != c) | (layer != l))(
                 lambda: trace_copy(z, col, layer).start())
 
     middle = (last - 1) * CHUNKS
-    early = [b for b, _ in from_right[0][:middle]].count(last) == CHUNKS
-
-    def partner(b, row):
-        return (b * per // n_layer) ^ (row * per // n_layer)
-
-    def diagonal(row):
-        @pl.when(on_diagonal & (r == row))
-        def _():
-            pairs = [0] + list(range(row + 1, n_row)) if row else [last] if early else []
-            add_trace([] if row == last else pairs, True)
-            if row > 0 or early:
+    pairs = {row: list(range(max(row + 1, 2 - row), n_row)) for row in range(n_row)}
+    pairs[1] += [0]
+    asked = list(range(1, n_row))
+
+    def ready_rows(count, distances):
+        def at_hand(b, row):
+            arrived = (from_left if b < row else from_right)[row][:count]
+            apart = (b * per // n_layer) ^ (row * per // n_layer)
+            return ([x for x, _ in arrived].count(b) == CHUNKS
+                    and (apart in distances or not relayed))
+
+        return [row for row in asked if all(at_hand(b, row) for b in pairs[row])]
+
+    def diagonals(chosen):
+        for row in chosen:
+            asked.remove(row)
+
+            @pl.when(on_diagonal & (r == row))
+            def _():
+                add_trace(pairs[row], True)
                 send_trace(row)
+                for copy, plan, sent, hold in (
+                        (to_left, leftward, sent_left, hold_left),
+                        (to_right, rightward, sent_right, hold_right)):
+                    if row in hold:
+                        for block, q in plan[row][hold[row]:sent[row]]:
+                            copy(block, q, row_panel.at[me, span(q)] if block == row
+                                 else col_panel.at[block, span(q)]).start()
+            hold_left.pop(row, None)
+            hold_right.pop(row, None)
 
     pl.when(has_left)(lambda: pl.semaphore_wait(ready.at[2], 1))
     pl.when(has_right)(lambda: answer(2, (right, c, l)))
     for other in layer_peers:
         side_wait(c * n_layer + other)
-    diagonal(last)
+    pl.when(on_diagonal & (r == 0))(lambda: add_trace([], True))
+    diagonals(ready_rows(0, ()))
     for k in range(CHUNKS // 2):
         z_arrive(k)
     for d in direct:
@@ -321,34 +342,24 @@
         z_arrive(k)
     for d in direct:
         plane_arrive(d, 1)
-    soon = CHUNKS + 1
-    for k in range(CHUNKS, soon):
+    for k in range(CHUNKS, CHUNKS + 1):
         z_arrive(k)
     for other in layer_peers:
         for d in direct:
             side_wait(col_peers[d - 1] * n_layer + other)
-    def needs(row):
-        blocks = {0: [last], last: []}.get(row, [0] + list(range(row + 1, n_row)))
-        late = [b for b in blocks if partner(b, row) in relayed]
-        for b in blocks:
-            arrived = (from_left if b < row else from_right)[row][:soon]
-            late += [b] if [x for x, _ in arrived].count(b) < CHUNKS else []
-        return late
-
-    quick = [row for row in range(1, last) if not needs(row)]
-    for row in quick:
-        diagonal(row)
+    diagonals(ready_rows(CHUNKS + 1, direct))
+    for k in range(CHUNKS + 1, CHUNKS + 2):
+        z_arrive(k)
     for turn in range(2):
         for d in relayed:
             plane_arrive(d, turn)
-    for k in range(soon, middle):
-        z_arrive(k)
     for other in layer_peers:
         for d in relayed:
             side_wait(col_peers[d - 1] * n_layer + other)
-    for row in range(last):
-        if row not in quick:
-            diagonal(row)
+    diagonals(ready_rows(CHUNKS + 2, range(n_col)))
+    for k in range(CHUNKS + 2, middle):
+        z_arrive(k)
+    diagonals(list(asked))
 
     total = None
     for t in range(per):
@@ -366,19 +377,18 @@
         def _():
             products = []
             for block in range(n_row):
-                held = sorted(q for b, q in arrived[:middle] if b == block)
-                if held:
-                    assert held == list(range(len(held)))
-                    products += terms(block, 0, len(held) * piece)
+                chunks = sorted(q for b, q in arrived[:middle] if b == block)
+                if chunks:
+                    assert chunks == list(range(len(chunks)))
+                    products += terms(block, 0, len(chunks) * piece)
             add(products)
 
     def finish(row, arrived, k):
         block, q = arrived[k]
-        held = [b for b, _ in arrived[:k + 1]].count(last)
-        if row == 0 and block == last and held == CHUNKS and not early:
+        if row == 0 and k == last * CHUNKS - 2:
             @pl.when(on_diagonal)
             def _():
-                add_trace([last], False)
+                add_trace(pairs[0], False)
                 send_trace(0)
         add(terms(block, q * piece, piece))
 
@@ -393,47 +403,6 @@
             doubled = 2.0 * row_panel[(me,) + at].astype(jnp.float32) - product
             kept = jnp.full((blk, blk), keep_mask[k, i].astype(jnp.float32))
             updated[at] = jnp.where(flag, product, doubled) * kept
-
-    def heard(first, count, sem):
-        pltpu.make_async_remote_copy(
-            src_ref=trace_in.at[pl.ds(first, count)],
-            dst_ref=trace_in.at[pl.ds(first, count)],
-            send_sem=trace_send.at[0], recv_sem=trace_recv.at[sem],
-            device_id=(r, c, l), device_id_type=MESH,
-        ).wait_recv()
-
-    def hear(first, count, sem):
-        pl.when(on_diagonal & (me >= first) & (me < first + count))(
-            lambda: heard(first, count - 1, sem))
-        pl.when(jnp.logical_not(on_diagonal & (me >= first) & (me < first + count)))(
-            lambda: heard(first, count, sem))
-
-    def sum_of(first, count):
-        total = trace_in[first]
-        for slot in range(first + 1, first + count):
-            total = total + trace_in[slot]
-        return total
-
-    def sum_copy(n, target):
-        return pltpu.make_async_remote_copy(
-            src_ref=trace_sum.at[n], dst_ref=trace_sum.at[0],
-            send_sem=sum_send.at[n], recv_sem=sum_recv.at[0],
-            device_id=(target, c, l), device_id_type=MESH,
-        )
-
-    @pl.when(inner)
-    def _():
-        hear(per, slots - per, 1)
-
-    @pl.when(r == 1)
-    def _():
-        trace_sum[1] = sum_of(per, slots - per)
-        sum_copy(1, 0).start()
-
-    @pl.when(r == last - 1)
-    def _():
-        trace_sum[2] = sum_of(per, slots - 2 * per)
-        sum_copy(2, last).start()
 
     for row in range(n_row):
         @pl.when(r == row)
@@ -459,33 +428,21 @@
     sent_slots(n_col - 1, row_panel, plane_send)
     sent_slots((n_layer - 1) * n_col, row_panel, side_send)
 
-    hear(0, per, 0)
-
-    @pl.when(r == last)
-    def _():
-        hear(last * per, per, 1)
-
-    @pl.when(jnp.logical_not(inner))
-    def _():
-        sum_copy(1, 0).wait_recv()
-
-    @pl.when(inner)
-    def _():
-        lines[...] = sum_of(0, slots)
-
-    @pl.when(r == 0)
-    def _():
-        lines[...] = sum_of(0, per) + trace_sum[0]
-
-    @pl.when(r == last)
-    def _():
-        lines[...] = sum_of(0, per) + sum_of(last * per, per) + trace_sum[0]
-
-    pl.when(r == 1)(lambda: sum_copy(1, 0).wait_send())
-    pl.when(r == last - 1)(lambda: sum_copy(2, last).wait_send())
-    for row in range(n_row):
-        pl.when(on_diagonal & (r == row))(
-            lambda: sent_slots(len(heirs(row)) - 1, trace_in, trace_send))
+    def heard(count):
+        pltpu.make_async_remote_copy(
+            src_ref=trace_in.at[pl.ds(0, count)], dst_ref=trace_in.at[pl.ds(0, count)],
+            send_sem=trace_send.at[0], recv_sem=trace_recv.at[0],
+            device_id=(r, c, l), device_id_type=MESH,
+        ).wait_recv()
+
+    pl.when(on_diagonal)(lambda: heard(slots - 1))
+    pl.when(jnp.logical_not(on_diagonal))(lambda: heard(slots))
+    parts = trace_in[0]
+    for slot in range(1, slots):
+        parts = parts + trace_in[slot]
+    lines[...] = parts
+    pl.when(on_diagonal)(
+        lambda: sent_slots(n_row * slots - 1, trace_in, trace_send))
 
 
 def deliver(updated, lines, out, trace):
@@ -527,9 +484,6 @@
             dma((1,)),
             dma((n_row, CHUNKS)),
             dma((1,)),
-            dma((2,)),
-            pltpu.VMEM((3, 3, blk), jnp.float32),
-            dma((3,)),
             dma((1,)),
             pltpu.SemaphoreType.REGULAR((3,)),
         ],

time: 26.5 us -> 25.1 us (0.947)
  Pallas kernels: 25.7 us -> 24.3 us
    pallas_call x1, Pallas kernels: 24.8 us -> 23.5 us  [on_device(): pl.pallas_call(functools.partial(kernel, sizes), out_shape=(jax.ShapeDtyp...]
where the time goes in v2:
time: 25.1 us; the launch traced here: 25 us
  Pallas kernels  24.3 us (97%)
  between operations  0.64 us (3%)
    pallas_call x1, Pallas kernels, on_device(): pl.pallas_call(functools.partial(kernel, sizes), out_shape=(jax.ShapeDtyp...  23.5 us
    pallas_call x1, Pallas kernels, on_device(): pl.pallas_call(deliver, out_shape=(jax.ShapeDtypeStruct((rows, width), jn...  0.84 us

profile of v2, /device:TPU:0, one launch (start us, length us, event | category | flops | bytes accessed | tf_op | source)
XLA Modules:
  0.0 25.0 jit_solution(7527322752925212465)
XLA Ops:
  0.6 23.5 %shard_map.59 = (f32[512,256]{1,0:T(8,128)S(1)}, f32[3,128]{1,0:T(4,128)S(1)}) custom-call(bf16[512,256]{1,0:T(8,128)(2,1)} %density_hbm.1, s32[2,4]{1,0:T(2,128)} %bitcast.3, s32[2,4]{1,0:T(2,128)} %bitcast.4, s32[4]{0:T(128)} %flag_hbm.1), custom_call_target="tpu_custom_call" | custom-call | tf_op jit(solution)/shard_map/pallas_call | solution.py:462
  24.1 0.8 %shard_map.60 = (f32[512,256]{1,0:T(8,128)}, f32[1,1]{1,0:T(1,128)}) custom-call(f32[512,256]{1,0:T(8,128)S(1)} %get-tuple-element.6.updated, f32[3,128]{1,0:T(4,128)S(1)} %get-tuple-element.7.lines), custom_call_target="tpu_custom_call" | custom-call | tf_op jit(solution)/shard_map/pallas_call | solution.py:497

commit v3 on v2

--- a/solution.py
+++ b/solution.py
@@ -53,11 +53,15 @@
     plane_peers = [(p, q) for p in col_peers for q in range(n_layer)]
     plane_peers += [(c, q) for q in layer_peers]
 
+    def span(q):
+        return pl.ds(q * piece, piece)
+
     loads = [
         pltpu.make_async_copy(source, target, local_sem.at[i])
-        for i, (source, target) in enumerate([
-            (block_hbm, block_mask), (density_hbm, density),
-            (keep_hbm, keep_mask), (flag_hbm, branch_flag)])
+        for i, (source, target) in enumerate(
+            [(block_hbm, block_mask)]
+            + [(density_hbm.at[span(q)], density.at[span(q)]) for q in range(CHUNKS)]
+            + [(keep_hbm, keep_mask), (flag_hbm, branch_flag)])
     ]
     for load in loads:
         load.start()
@@ -79,17 +83,15 @@
     pl.when(has_left)(lambda: answer(0, (left, c, l)))
     for p, q in plane_peers:
         pl.when(p * n_layer + q < me)(functools.partial(answer, 1, (r, p, q)))
-    for load in loads:
-        load.wait()
-
-    for i in range(rows // blk):
-        for k in range(width // blk):
-            at = (pl.ds(i * blk, blk), pl.ds(k * blk, blk))
-            kept = jnp.full((blk, blk), block_mask[k, i].astype(jnp.float32))
-            row_panel[(me,) + at] = density[at] * kept.astype(jnp.bfloat16)
-
-    def span(q):
-        return pl.ds(q * piece, piece)
+    def mask(q):
+        loads[1 + q].wait()
+        for i in range(q * piece // blk, (q + 1) * piece // blk):
+            for k in range(width // blk):
+                at = (pl.ds(i * blk, blk), pl.ds(k * blk, blk))
+                kept = jnp.full((blk, blk), block_mask[k, i].astype(jnp.float32))
+                row_panel[(me,) + at] = density[at] * kept.astype(jnp.bfloat16)
+
+    loads[0].wait()
 
     def z_copy(block, q, source, target, sem):
         return pltpu.make_async_remote_copy(
@@ -171,10 +173,15 @@
 
     sent_left, sent_right = [0] * n_row, [0] * n_row
     hold_left, hold_right = {1: last * CHUNKS - 3}, {last - 1: 2 * CHUNKS - 1}
-    for row in range(1, n_row):
-        @pl.when(r == row)
-        def _():
-            sent_left[row] = pass_on(to_left, row, leftward[row], 0, (), AHEAD)
+    for q in range(CHUNKS):
+        mask(q)
+        for row in range(1, n_row) if q < AHEAD else []:
+            @pl.when(r == row)
+            def _():
+                sent_left[row] = pass_on(
+                    to_left, row, leftward[row], sent_left[row], (), q + 1)
+    for load in loads[1 + CHUNKS:]:
+        load.wait()
     plane_start(lambda peer: peer < c)
     pl.when(has_right)(lambda: pl.semaphore_wait(ready.at[0], 1))
     for row in range(last):
@@ -266,7 +273,7 @@
     everyone = [(z, col, layer) for z in range(n_row) for col in range(n_col)
                 for layer in range(n_layer)]
 
-    def add_trace(blocks, start):
+    def add_trace(chunks, start):
         weights = [weight(t, 1, -1) for t in range(tiles)]
         part = spread = others = jnp.zeros((1, blk), jnp.float32)
         if not start:
@@ -277,15 +284,15 @@
                 jnp.where(eye, own.astype(jnp.float32), 0.0), axis=0, keepdims=True)
             part += weight(t, 0, 2) * line
             spread += jnp.where(lanes == me * tiles + t, weights[t], 0.0)
-        for block in ([r] if start else []) + blocks:
-            for k in range(rows // blk):
-                sums = pair_sums(block, k)
-                for t in range(tiles):
-                    part += weights[t] * sums[t]
-                if block is not r:
-                    here = block * (rows // blk) + k
-                    total = sum(jnp.sum(line, keepdims=True) for line in sums)
-                    others += jnp.where(lanes == here, total, 0.0)
+        every = range(rows // blk)
+        for block, k in ([(r, k) for k in every] if start else []) + chunks:
+            sums = pair_sums(block, k)
+            for t in range(tiles):
+                part += weights[t] * sums[t]
+            if block is not r:
+                here = block * (rows // blk) + k
+                total = sum(jnp.sum(line, keepdims=True) for line in sums)
+                others += jnp.where(lanes == here, total, 0.0)
         trace_own[0:1, :] = part
         trace_own[1:2, :] = spread
         trace_own[2:3, :] = others
@@ -316,7 +323,7 @@
 
             @pl.when(on_diagonal & (r == row))
             def _():
-                add_trace(pairs[row], True)
+                add_trace([(b, k) for b in pairs[row] for k in range(rows // blk)], True)
                 send_trace(row)
                 for copy, plan, sent, hold in (
                         (to_left, leftward, sent_left, hold_left),
@@ -385,13 +392,20 @@
 
     def finish(row, arrived, k):
         block, q = arrived[k]
-        if row == 0 and k == last * CHUNKS - 2:
+        if row == 0 and block in pairs[0]:
             @pl.when(on_diagonal)
             def _():
-                add_trace(pairs[0], False)
-                send_trace(0)
+                add_trace(parts_of([(block, q)]), False)
+                if k == last * CHUNKS - 2:
+                    send_trace(0)
         add(terms(block, q * piece, piece))
 
+    def parts_of(chunks):
+        share = piece // blk
+        return [(b, q * share + k) for b, q in chunks if b in pairs[0] for k in range(share)]
+
+    pl.when(on_diagonal & (r == 0))(
+        lambda: add_trace(parts_of(from_right[0][:middle]), False))
     for k in range(middle, last * CHUNKS):
         z_arrive(k, finish)
 
@@ -476,7 +490,7 @@
             pltpu.VMEM((n_row, rows, width), jnp.bfloat16),
             pltpu.VMEM((3, blk), jnp.float32),
             pltpu.VMEM((n_row * slots, 3, blk), jnp.float32),
-            dma((4,)),
+            dma((CHUNKS + 3,)),
             dma((1,)),
             dma((slots, 2)),
             dma((1,)),

time: 25.1 us -> 24.7 us (0.984)
  Pallas kernels: 24.3 us -> 23.9 us
    pallas_call x1, Pallas kernels: 23.5 us -> 23 us  [on_device(): pl.pallas_call(functools.partial(kernel, sizes), out_shape=(jax.ShapeDtyp...]
where the time goes in v3:
time: 24.7 us; the launch traced here: 24.5 us
  Pallas kernels  23.9 us (97%)
  between operations  0.64 us (3%)
    pallas_call x1, Pallas kernels, on_device(): pl.pallas_call(functools.partial(kernel, sizes), out_shape=(jax.ShapeDtyp...  23 us
    pallas_call x1, Pallas kernels, on_device(): pl.pallas_call(deliver, out_shape=(jax.ShapeDtypeStruct((rows, width), jn...  0.84 us

profile of v3, /device:TPU:0, one launch (start us, length us, event | category | flops | bytes accessed | tf_op | source)
XLA Modules:
  0.0 24.5 jit_solution(5450141280606089868)
XLA Ops:
  0.6 23.0 %shard_map.59 = (f32[512,256]{1,0:T(8,128)S(1)}, f32[3,128]{1,0:T(4,128)S(1)}) custom-call(bf16[512,256]{1,0:T(8,128)(2,1)} %density_hbm.1, s32[2,4]{1,0:T(2,128)} %bitcast.3, s32[2,4]{1,0:T(2,128)} %bitcast.4, s32[4]{0:T(128)} %flag_hbm.1), custom_call_target="tpu_custom_call" | custom-call | tf_op jit(solution)/shard_map/pallas_call | solution.py:476
  23.7 0.8 %shard_map.60 = (f32[512,256]{1,0:T(8,128)}, f32[1,1]{1,0:T(1,128)}) custom-call(f32[512,256]{1,0:T(8,128)S(1)} %get-tuple-element.6.updated, f32[3,128]{1,0:T(4,128)S(1)} %get-tuple-element.7.lines), custom_call_target="tpu_custom_call" | custom-call | tf_op jit(solution)/shard_map/pallas_call | solution.py:511

commit v4 on v3

--- a/solution.py
+++ b/solution.py
@@ -35,7 +35,7 @@
     density, block_mask, keep_mask, branch_flag,
     row_panel, col_panel, trace_own, trace_in, local_sem,
     plane_send, plane_recv, side_send, right_send, left_send, z_recv,
-    trace_send, trace_recv, ready,
+    trace_send, trace_recv, trace_swap, trace_sum, ready,
 ):
     n_row, n_col, n_layer = sizes
     rows, width = density.shape
@@ -270,6 +270,43 @@
             device_id=(z, col, layer), device_id_type=MESH,
         )
 
+    assert per % n_layer == 0
+    firsts = per // n_layer
+
+    def swap_copy(other):
+        return pltpu.make_async_remote_copy(
+            src_ref=trace_own, dst_ref=trace_swap.at[l],
+            send_sem=trace_send.at[0], recv_sem=trace_recv.at[1],
+            device_id=(r, c, other), device_id_type=MESH,
+        )
+
+    def sum_copy(z, col):
+        return pltpu.make_async_remote_copy(
+            src_ref=trace_sum, dst_ref=trace_in.at[me],
+            send_sem=trace_send.at[0], recv_sem=trace_recv.at[0],
+            device_id=(z, col, l), device_id_type=MESH,
+        )
+
+    def send_first():
+        trace_swap[l] = trace_own[...]
+        for other in layer_peers:
+            swap_copy(other).start()
+        if n_layer > 1:
+            pltpu.make_async_remote_copy(
+                src_ref=trace_in.at[pl.ds(0, n_layer - 1)],
+                dst_ref=trace_in.at[pl.ds(0, n_layer - 1)],
+                send_sem=trace_send.at[0], recv_sem=trace_recv.at[1],
+                device_id=(r, c, l), device_id_type=MESH,
+            ).wait_recv()
+        total = trace_swap[0]
+        for layer in range(1, n_layer):
+            total = total + trace_swap[layer]
+        trace_sum[...] = total
+        trace_in[me] = total
+        for z in range(n_row - 1, -1, -1):
+            for col in range(n_col):
+                pl.when((z != r) | (col != c))(lambda: sum_copy(z, col).start())
+
     everyone = [(z, col, layer) for z in range(n_row) for col in range(n_col)
                 for layer in range(n_layer)]
 
@@ -351,21 +388,24 @@
         plane_arrive(d, 1)
     for k in range(CHUNKS, CHUNKS + 1):
         z_arrive(k)
-    for other in layer_peers:
-        for d in direct:
-            side_wait(col_peers[d - 1] * n_layer + other)
-    diagonals(ready_rows(CHUNKS + 1, direct))
+    def sides(chosen):
+        for other in layer_peers:
+            for d in chosen:
+                side_wait(col_peers[d - 1] * n_layer + other)
+
+    soon = ready_rows(CHUNKS + 1, direct)
+    in_soon = functools.reduce(jnp.logical_or, [r == row for row in soon], r < 0)
+    pl.when(in_soon)(lambda: sides(direct))
+    diagonals(soon)
     for k in range(CHUNKS + 1, CHUNKS + 2):
         z_arrive(k)
     for turn in range(2):
         for d in relayed:
             plane_arrive(d, turn)
-    for other in layer_peers:
-        for d in relayed:
-            side_wait(col_peers[d - 1] * n_layer + other)
-    diagonals(ready_rows(CHUNKS + 2, range(n_col)))
     for k in range(CHUNKS + 2, middle):
         z_arrive(k)
+    pl.when(jnp.logical_not(in_soon))(lambda: sides(direct))
+    sides(relayed)
     diagonals(list(asked))
 
     total = None
@@ -397,8 +437,23 @@
             def _():
                 add_trace(parts_of([(block, q)]), False)
                 if k == last * CHUNKS - 2:
-                    send_trace(0)
-        add(terms(block, q * piece, piece))
+                    send_first()
+        if k < last * CHUNKS - 1:
+            add(terms(block, q * piece, piece))
+        else:
+            update(terms(block, q * piece, piece))
+
+    def update(products):
+        for i in range(rows // blk):
+            flag = jnp.full((blk, blk), branch_flag[i]) == 1
+            for k in range(width // blk):
+                at = (pl.ds(i * blk, blk), pl.ds(k * blk, blk))
+                square = updated[at]
+                for product in products:
+                    square += product[i * blk:(i + 1) * blk, k * blk:(k + 1) * blk]
+                doubled = 2.0 * row_panel[(me,) + at].astype(jnp.float32) - square
+                kept = jnp.full((blk, blk), keep_mask[k, i].astype(jnp.float32))
+                updated[at] = jnp.where(flag, square, doubled) * kept
 
     def parts_of(chunks):
         share = piece // blk
@@ -409,14 +464,7 @@
     for k in range(middle, last * CHUNKS):
         z_arrive(k, finish)
 
-    for i in range(rows // blk):
-        flag = jnp.full((blk, blk), branch_flag[i]) == 1
-        for k in range(width // blk):
-            at = (pl.ds(i * blk, blk), pl.ds(k * blk, blk))
-            product = updated[at]
-            doubled = 2.0 * row_panel[(me,) + at].astype(jnp.float32) - product
-            kept = jnp.full((blk, blk), keep_mask[k, i].astype(jnp.float32))
-            updated[at] = jnp.where(flag, product, doubled) * kept
+    pl.when(inner)(lambda: update([]))
 
     for row in range(n_row):
         @pl.when(r == row)
@@ -449,14 +497,18 @@
             device_id=(r, c, l), device_id_type=MESH,
         ).wait_recv()
 
-    pl.when(on_diagonal)(lambda: heard(slots - 1))
-    pl.when(jnp.logical_not(on_diagonal))(lambda: heard(slots))
-    parts = trace_in[0]
-    for slot in range(1, slots):
+    pl.when(on_diagonal)(lambda: heard(slots - per + firsts - 1))
+    pl.when(jnp.logical_not(on_diagonal))(lambda: heard(slots - per + firsts))
+    parts = trace_in[l]
+    for slot in range(1, firsts):
+        parts = parts + trace_in[slot * n_layer + l]
+    for slot in range(per, slots):
         parts = parts + trace_in[slot]
     lines[...] = parts
-    pl.when(on_diagonal)(
+    pl.when(on_diagonal & has_left)(
         lambda: sent_slots(n_row * slots - 1, trace_in, trace_send))
+    pl.when(on_diagonal & jnp.logical_not(has_left))(
+        lambda: sent_slots(n_row * n_col + n_layer - 2, trace_in, trace_send))
 
 
 def deliver(updated, lines, out, trace):
@@ -498,7 +550,9 @@
             dma((1,)),
             dma((n_row, CHUNKS)),
             dma((1,)),
-            dma((1,)),
+            dma((2,)),
+            pltpu.VMEM((n_layer, 3, blk), jnp.float32),
+            pltpu.VMEM((3, blk), jnp.float32),
             pltpu.SemaphoreType.REGULAR((3,)),
         ],
         compiler_params=pltpu.CompilerParams(

time: 24.7 us -> 24.6 us (level)
  no operation moved by 1% of the time
where the time goes in v4:
time: 24.6 us; the launch traced here: 24.3 us
  Pallas kernels  23.7 us (96%)
  between operations  0.64 us (3%)
    pallas_call x1, Pallas kernels, on_device(): pl.pallas_call(functools.partial(kernel, sizes), out_shape=(jax.ShapeDtyp...  22.9 us
    pallas_call x1, Pallas kernels, on_device(): pl.pallas_call(deliver, out_shape=(jax.ShapeDtypeStruct((rows, width), jn...  0.84 us

profile of v4, /device:TPU:0, one launch (start us, length us, event | category | flops | bytes accessed | tf_op | source)
XLA Modules:
  0.0 24.3 jit_solution(16944190020070176954)
XLA Ops:
  0.6 22.9 %shard_map.59 = (f32[512,256]{1,0:T(8,128)S(1)}, f32[3,128]{1,0:T(4,128)S(1)}) custom-call(bf16[512,256]{1,0:T(8,128)(2,1)} %density_hbm.1, s32[2,4]{1,0:T(2,128)} %bitcast.3, s32[2,4]{1,0:T(2,128)} %bitcast.4, s32[4]{0:T(128)} %flag_hbm.1), custom_call_target="tpu_custom_call" | custom-call | tf_op jit(solution)/shard_map/pallas_call | solution.py:528
  23.5 0.8 %shard_map.60 = (f32[512,256]{1,0:T(8,128)}, f32[1,1]{1,0:T(1,128)}) custom-call(f32[512,256]{1,0:T(8,128)S(1)} %get-tuple-element.6.updated, f32[3,128]{1,0:T(4,128)S(1)} %get-tuple-element.7.lines), custom_call_target="tpu_custom_call" | custom-call | tf_op jit(solution)/shard_map/pallas_call | solution.py:565

commit v5 on v4

--- a/solution.py
+++ b/solution.py
@@ -35,7 +35,7 @@
     density, block_mask, keep_mask, branch_flag,
     row_panel, col_panel, trace_own, trace_in, local_sem,
     plane_send, plane_recv, side_send, right_send, left_send, z_recv,
-    trace_send, trace_recv, trace_swap, trace_sum, ready,
+    trace_send, trace_recv, trace_swap, trace_sum, aside, aside_send, aside_sems, ready,
 ):
     n_row, n_col, n_layer = sizes
     rows, width = density.shape
@@ -50,8 +50,23 @@
     left, right = jnp.maximum(r - 1, 0), jnp.minimum(r + 1, last)
     col_peers = [partner_of(c, d, n_col) for d in range(1, n_col)]
     layer_peers = [partner_of(l, d, n_layer) for d in range(1, n_layer)]
-    plane_peers = [(p, q) for p in col_peers for q in range(n_layer)]
-    plane_peers += [(c, q) for q in layer_peers]
+
+    bits = [d for d in range(1, n_col) if d & (d - 1) == 0]
+    relayed = [lo | hi for hi in bits for lo in bits if lo < hi]
+    if n_col & (n_col - 1):
+        bits, relayed = list(range(1, n_col)), []
+    direct = [d for d in range(1, n_col) if d not in relayed]
+    halves = {d: (1, 0) if relayed and d > 1 else (0, 1) for d in range(1, n_col)}
+
+    plane_peers = [(c, q, True, 1) for q in layer_peers]
+    for d in range(1, n_col):
+        p = col_peers[d - 1]
+        met = (p * c == 0) if d in relayed and len(bits) == 2 else True
+        plane_peers += [(p, q, met, 3 if d in relayed else 1) for q in range(n_layer)]
+
+    def counted(which, above):
+        return sum(jnp.where(((p * n_layer + q > me) == above) & met, 1, 0)
+                   for p, q, met, to in plane_peers if to in which)
 
     def span(q):
         return pl.ds(q * piece, piece)
@@ -76,13 +91,13 @@
             ready.at[which], inc=1, device_id=target, device_id_type=MESH)
 
     pl.when(has_right)(lambda: greet((right, c, l)))
-    for p, q in plane_peers:
-        pl.when(p * n_layer + q > me)(functools.partial(greet, (r, p, q)))
-    below, above = jnp.where(has_left, 1, 0) + me, slots - 1 - me
+    for p, q, met, _ in plane_peers:
+        pl.when((p * n_layer + q > me) & met)(functools.partial(greet, (r, p, q)))
+    below = jnp.where(has_left, 1, 0) + counted((1, 3), False)
     pl.when(below > 0)(lambda: pl.semaphore_wait(barrier, below))
     pl.when(has_left)(lambda: answer(0, (left, c, l)))
-    for p, q in plane_peers:
-        pl.when(p * n_layer + q < me)(functools.partial(answer, 1, (r, p, q)))
+    for p, q, met, to in plane_peers:
+        pl.when((p * n_layer + q < me) & met)(functools.partial(answer, to, (r, p, q)))
     def mask(q):
         loads[1 + q].wait()
         for i in range(q * piece // blk, (q + 1) * piece // blk):
@@ -124,13 +139,6 @@
     def side_wait(slot):
         for h in range(2):
             half_copy(slot, h, side_send, (r, c, l)).wait_recv()
-
-    bits = [d for d in range(1, n_col) if d & (d - 1) == 0]
-    relayed = [lo | hi for hi in bits for lo in bits if lo < hi]
-    if n_col & (n_col - 1):
-        bits, relayed = list(range(1, n_col)), []
-    direct = [d for d in range(1, n_col) if d not in relayed]
-    halves = {d: (1, 0) if relayed and d > 1 else (0, 1) for d in range(1, n_col)}
 
     def plane_start(chosen):
         for turn in range(2):
@@ -153,6 +161,32 @@
     from_right = leftward[1:] + [[]]
 
     on_diagonal = me // per == r
+
+    detour = bool(relayed) and n_layer <= len(bits)
+    by_way = functools.reduce(jnp.logical_or, [
+        (l == layer) & (c == bits[layer]) for layer in range(n_layer if detour else 0)],
+        c < 0)
+
+    def detour_copy(source, target, column, row, sem, recv):
+        return pltpu.make_async_remote_copy(
+            src_ref=source, dst_ref=target, send_sem=sem.at[0], recv_sem=recv,
+            device_id=(row, column, l), device_id_type=MESH,
+        )
+
+    def detour_start():
+        for layer in range(n_layer):
+            pl.when((r == 1) & (c == 0) & (l == layer))(detour_copy(
+                row_panel.at[me, span(CHUNKS - 1)], aside, bits[layer], 1,
+                left_send, aside_sems.at[0]).start)
+
+    def detour_pass(row):
+        target, recv = ((aside, aside_sems.at[0]) if row else
+                        (col_panel.at[1, span(CHUNKS - 1)], z_recv.at[1, CHUNKS - 1]))
+
+        @pl.when(by_way & (r == row))
+        def _():
+            detour_copy(aside, aside, c, 0, aside_send, aside_sems.at[0]).wait_recv()
+            detour_copy(aside, target, c if row else 0, 0, aside_send, recv).start()
 
     def pass_on(copy, row, plan, first, arrived, stop=None, hold=None):
         while first < len(plan) and (stop is None or first < stop):
@@ -163,7 +197,10 @@
                 source = col_panel.at[block, span(q)]
             else:
                 break
-            if hold is None or first < hold:
+            if detour and copy is to_left and (row, block, q) == (1, 1, CHUNKS - 1):
+                pl.when(jnp.logical_not(on_diagonal) & (c > 0))(
+                    functools.partial(lambda f: f.start(), copy(block, q, source)))
+            elif hold is None or first < hold:
                 copy(block, q, source).start()
             else:
                 pl.when(jnp.logical_not(on_diagonal))(
@@ -172,7 +209,7 @@
         return first
 
     sent_left, sent_right = [0] * n_row, [0] * n_row
-    hold_left, hold_right = {1: last * CHUNKS - 3}, {last - 1: 2 * CHUNKS - 1}
+    hold_left, hold_right = {1: last * CHUNKS - 2}, {last - 1: 2 * CHUNKS - 1}
     for q in range(CHUNKS):
         mask(q)
         for row in range(1, n_row) if q < AHEAD else []:
@@ -188,15 +225,19 @@
         @pl.when(r == row)
         def _():
             sent_right[row] = pass_on(to_right, row, rightward[row], 0, (), AHEAD)
-    pl.when(above > 0)(lambda: pl.semaphore_wait(ready.at[1], above))
+    near_above, far_above = counted((1,), True), counted((3,), True)
+    pl.when(near_above > 0)(lambda: pl.semaphore_wait(ready.at[1], near_above))
     for row in range(n_row):
         @pl.when(r == row)
         def _():
             sent_left[row] = pass_on(
-                to_left, row, leftward[row], sent_left[row], (), None, hold_left.get(row))
+                to_left, row, leftward[row], sent_left[row], (),
+                CHUNKS - 1 if row == last else None, hold_left.get(row))
             sent_right[row] = pass_on(
                 to_right, row, rightward[row], sent_right[row], (), None, hold_right.get(row))
     plane_start(lambda peer: peer > c)
+    if detour:
+        detour_start()
     for h in range(2):
         side_copies(me, h)
 
@@ -372,6 +413,10 @@
             hold_left.pop(row, None)
             hold_right.pop(row, None)
 
+    pl.when(far_above > 0)(lambda: pl.semaphore_wait(ready.at[3], far_above))
+    @pl.when(r == last)
+    def _():
+        sent_left[last] = pass_on(to_left, last, leftward[last], sent_left[last], ())
     pl.when(has_left)(lambda: pl.semaphore_wait(ready.at[2], 1))
     pl.when(has_right)(lambda: answer(2, (right, c, l)))
     for other in layer_peers:
@@ -397,6 +442,8 @@
     in_soon = functools.reduce(jnp.logical_or, [r == row for row in soon], r < 0)
     pl.when(in_soon)(lambda: sides(direct))
     diagonals(soon)
+    if detour:
+        detour_pass(1)
     for k in range(CHUNKS + 1, CHUNKS + 2):
         z_arrive(k)
     for turn in range(2):
@@ -459,6 +506,8 @@
         share = piece // blk
         return [(b, q * share + k) for b, q in chunks if b in pairs[0] for k in range(share)]
 
+    if detour:
+        detour_pass(0)
     pl.when(on_diagonal & (r == 0))(
         lambda: add_trace(parts_of(from_right[0][:middle]), False))
     for k in range(middle, last * CHUNKS):
@@ -466,6 +515,9 @@
 
     pl.when(inner)(lambda: update([]))
 
+    if detour:
+        pl.when(by_way & (r < 2))(
+            detour_copy(aside, aside, c, 0, aside_send, aside_sems.at[0]).wait_send)
     for row in range(n_row):
         @pl.when(r == row)
         def _():
@@ -553,7 +605,10 @@
             dma((2,)),
             pltpu.VMEM((n_layer, 3, blk), jnp.float32),
             pltpu.VMEM((3, blk), jnp.float32),
-            pltpu.SemaphoreType.REGULAR((3,)),
+            pltpu.VMEM((rows // CHUNKS, width), jnp.bfloat16),
+            dma((1,)),
+            dma((1,)),
+            pltpu.SemaphoreType.REGULAR((4,)),
         ],
         compiler_params=pltpu.CompilerParams(
             collective_id=0, has_side_effects=True,

time: 24.6 us -> 24.1 us (0.980)
  Pallas kernels: 23.7 us -> 23.3 us
    pallas_call x1, Pallas kernels: 22.9 us -> 22.5 us  [on_device(): pl.pallas_call(functools.partial(kernel, sizes), out_shape=(jax.ShapeDtyp...]
where the time goes in v5:
time: 24.1 us; the launch traced here: 24 us
  Pallas kernels  23.3 us (97%)
  between operations  0.64 us (3%)
    pallas_call x1, Pallas kernels, on_device(): pl.pallas_call(functools.partial(kernel, sizes), out_shape=(jax.ShapeDtyp...  22.5 us
    pallas_call x1, Pallas kernels, on_device(): pl.pallas_call(deliver, out_shape=(jax.ShapeDtypeStruct((rows, width), jn...  0.84 us

profile of v5, /device:TPU:0, one launch (start us, length us, event | category | flops | bytes accessed | tf_op | source)
XLA Modules:
  0.0 24.0 jit_solution(5905759255919630479)
XLA Ops:
  0.6 22.5 %shard_map.59 = (f32[512,256]{1,0:T(8,128)S(1)}, f32[3,128]{1,0:T(4,128)S(1)}) custom-call(bf16[512,256]{1,0:T(8,128)(2,1)} %density_hbm.1, s32[2,4]{1,0:T(2,128)} %bitcast.3, s32[2,4]{1,0:T(2,128)} %bitcast.4, s32[4]{0:T(128)} %flag_hbm.1), custom_call_target="tpu_custom_call" | custom-call | tf_op jit(solution)/shard_map/pallas_call | solution.py:580
  23.1 0.8 %shard_map.60 = (f32[512,256]{1,0:T(8,128)}, f32[1,1]{1,0:T(1,128)}) custom-call(f32[512,256]{1,0:T(8,128)S(1)} %get-tuple-element.6.updated, f32[3,128]{1,0:T(4,128)S(1)} %get-tuple-element.7.lines), custom_call_target="tpu_custom_call" | custom-call | tf_op jit(solution)/shard_map/pallas_call | solution.py:620

commit v6 on v5

--- a/solution.py
+++ b/solution.py
@@ -34,7 +34,7 @@
     sizes, density_hbm, block_hbm, keep_hbm, flag_hbm, updated, lines,
     density, block_mask, keep_mask, branch_flag,
     row_panel, col_panel, trace_own, trace_in, local_sem,
-    plane_send, plane_recv, side_send, right_send, left_send, z_recv,
+    plane_send, plane_recv, side_send, side_recv, right_send, left_send, z_recv,
     trace_send, trace_recv, trace_swap, trace_sum, aside, aside_send, aside_sems, ready,
 ):
     n_row, n_col, n_layer = sizes
@@ -121,40 +121,46 @@
     def to_left(block, q, source):
         return z_copy(block, q, source, left, left_send)
 
-    def half_copy(slot, h, sem, target):
+    def half_copy(slot, h, sem, recv, target):
         half = pl.ds(h * (rows // 2), rows // 2)
         return pltpu.make_async_remote_copy(
             src_ref=row_panel.at[slot, half], dst_ref=row_panel.at[slot, half],
-            send_sem=sem.at[0], recv_sem=plane_recv.at[slot, h],
-            device_id=target, device_id_type=MESH,
+            send_sem=sem.at[0], recv_sem=recv, device_id=target, device_id_type=MESH,
         )
 
-    def plane_copy(slot, h, peer):
-        return half_copy(slot, h, plane_send, (r, peer, l))
-
-    def side_copies(slot, h):
+    def plane_copy(slot, h, d, peer):
+        return half_copy(slot, h, plane_send, plane_recv.at[d - 1, h], (r, peer, l))
+
+    def side_copies(slot, h, group):
         for other in layer_peers:
-            half_copy(slot, h, side_send, (r, c, other)).start()
-
-    def side_wait(slot):
-        for h in range(2):
-            half_copy(slot, h, side_send, (r, c, l)).wait_recv()
+            half_copy(slot, h, side_send, side_recv.at[group], (r, c, other)).start()
+
+    def side_wait(count, group):
+        blocks = row_panel.at[pl.ds(0, count)]
+        if count:
+            pltpu.make_async_remote_copy(
+                src_ref=blocks, dst_ref=blocks, send_sem=side_send.at[0],
+                recv_sem=side_recv.at[group], device_id=(r, c, l), device_id_type=MESH,
+            ).wait_recv()
+
+    def seen(d):
+        return n_col - d if n_col & (n_col - 1) else d
 
     def plane_start(chosen):
         for turn in range(2):
             for d in direct:
                 peer = col_peers[d - 1]
                 pl.when(chosen(peer))(
-                    lambda: plane_copy(me, halves[d][turn], peer).start())
+                    lambda: plane_copy(me, halves[d][turn], seen(d), peer).start())
 
     def plane_arrive(d, turn):
         peer, h = col_peers[d - 1], halves[d][turn]
         slot = peer * n_layer + l
-        plane_copy(slot, h, peer).wait_recv()
+        plane_copy(slot, h, d, peer).wait_recv()
         for other in bits if relayed and d in bits else []:
             if (other > d) == (h == 0) and other != d:
-                plane_copy(slot, h, col_peers[other - 1]).start()
-        side_copies(slot, h)
+                plane_copy(slot, h, d | other, col_peers[other - 1]).start()
+        side_copies(slot, h, 2 if d in relayed else 1)
 
     rightward, leftward = passing_plans(n_row)
     from_left = [[]] + rightward[:-1]
@@ -235,11 +241,11 @@
                 CHUNKS - 1 if row == last else None, hold_left.get(row))
             sent_right[row] = pass_on(
                 to_right, row, rightward[row], sent_right[row], (), None, hold_right.get(row))
-    plane_start(lambda peer: peer > c)
     if detour:
         detour_start()
+    plane_start(lambda peer: peer > c)
     for h in range(2):
-        side_copies(me, h)
+        side_copies(me, h, 0)
 
     def z_arrive(k, then=None):
         for row in range(n_row):
@@ -321,11 +327,11 @@
             device_id=(r, c, other), device_id_type=MESH,
         )
 
-    def sum_copy(z, col):
+    def sum_copy(z, col, layer):
         return pltpu.make_async_remote_copy(
             src_ref=trace_sum, dst_ref=trace_in.at[me],
             send_sem=trace_send.at[0], recv_sem=trace_recv.at[0],
-            device_id=(z, col, l), device_id_type=MESH,
+            device_id=(z, col, layer), device_id_type=MESH,
         )
 
     def send_first():
@@ -344,9 +350,15 @@
             total = total + trace_swap[layer]
         trace_sum[...] = total
         trace_in[me] = total
-        for z in range(n_row - 1, -1, -1):
+        @pl.when(l == 0)
+        def _():
             for col in range(n_col):
-                pl.when((z != r) | (col != c))(lambda: sum_copy(z, col).start())
+                for layer in range(n_layer):
+                    sum_copy(last, col, layer).start()
+
+        for z in range(last - 1, -1, -1):
+            for col in range(n_col):
+                pl.when((z != r) | (col != c))(lambda: sum_copy(z, col, l).start())
 
     everyone = [(z, col, layer) for z in range(n_row) for col in range(n_col)
                 for layer in range(n_layer)]
@@ -419,8 +431,7 @@
         sent_left[last] = pass_on(to_left, last, leftward[last], sent_left[last], ())
     pl.when(has_left)(lambda: pl.semaphore_wait(ready.at[2], 1))
     pl.when(has_right)(lambda: answer(2, (right, c, l)))
-    for other in layer_peers:
-        side_wait(c * n_layer + other)
+    side_wait(n_layer - 1, 0)
     pl.when(on_diagonal & (r == 0))(lambda: add_trace([], True))
     diagonals(ready_rows(0, ()))
     for k in range(CHUNKS // 2):
@@ -429,26 +440,26 @@
         plane_arrive(d, 0)
     for k in range(CHUNKS // 2, CHUNKS):
         z_arrive(k)
+    if detour:
+        detour_pass(1)
     for d in direct:
         plane_arrive(d, 1)
     for k in range(CHUNKS, CHUNKS + 1):
         z_arrive(k)
     def sides(chosen):
-        for other in layer_peers:
-            for d in chosen:
-                side_wait(col_peers[d - 1] * n_layer + other)
+        side_wait(len(chosen) * (n_layer - 1), 2 if chosen is relayed else 1)
 
     soon = ready_rows(CHUNKS + 1, direct)
     in_soon = functools.reduce(jnp.logical_or, [r == row for row in soon], r < 0)
     pl.when(in_soon)(lambda: sides(direct))
     diagonals(soon)
-    if detour:
-        detour_pass(1)
     for k in range(CHUNKS + 1, CHUNKS + 2):
         z_arrive(k)
     for turn in range(2):
         for d in relayed:
             plane_arrive(d, turn)
+    if detour:
+        detour_pass(0)
     for k in range(CHUNKS + 2, middle):
         z_arrive(k)
     pl.when(jnp.logical_not(in_soon))(lambda: sides(direct))
@@ -506,8 +517,6 @@
         share = piece // blk
         return [(b, q * share + k) for b, q in chunks if b in pairs[0] for k in range(share)]
 
-    if detour:
-        detour_pass(0)
     pl.when(on_diagonal & (r == 0))(
         lambda: add_trace(parts_of(from_right[0][:middle]), False))
     for k in range(middle, last * CHUNKS):
@@ -551,16 +560,19 @@
 
     pl.when(on_diagonal)(lambda: heard(slots - per + firsts - 1))
     pl.when(jnp.logical_not(on_diagonal))(lambda: heard(slots - per + firsts))
-    parts = trace_in[l]
+    giver = jnp.where(r == last, 0, l)
+    parts = trace_in[giver]
     for slot in range(1, firsts):
-        parts = parts + trace_in[slot * n_layer + l]
+        parts = parts + trace_in[slot * n_layer + giver]
     for slot in range(per, slots):
         parts = parts + trace_in[slot]
     lines[...] = parts
     pl.when(on_diagonal & has_left)(
         lambda: sent_slots(n_row * slots - 1, trace_in, trace_send))
-    pl.when(on_diagonal & jnp.logical_not(has_left))(
-        lambda: sent_slots(n_row * n_col + n_layer - 2, trace_in, trace_send))
+    first_sent = last * n_col + n_layer - 2
+    for core, count in ((l == 0, first_sent + n_col * n_layer), (l > 0, first_sent)):
+        pl.when(on_diagonal & jnp.logical_not(has_left) & core)(
+            functools.partial(sent_slots, count, trace_in, trace_send))
 
 
 def deliver(updated, lines, out, trace):
@@ -596,8 +608,9 @@
             pltpu.VMEM((n_row * slots, 3, blk), jnp.float32),
             dma((CHUNKS + 3,)),
             dma((1,)),
-            dma((slots, 2)),
+            dma((max(n_col - 1, 1), 2)),
             dma((1,)),
+            dma((3,)),
             dma((1,)),
             dma((1,)),
             dma((n_row, CHUNKS)),

time: 24.1 us -> 23.9 us (level)
  no operation moved by 1% of the time
where the time goes in v6:
time: 23.9 us; the launch traced here: 23.7 us
  Pallas kernels  23.1 us (97%)
  between operations  0.64 us (3%)
    pallas_call x1, Pallas kernels, on_device(): pl.pallas_call(functools.partial(kernel, sizes), out_shape=(jax.ShapeDtyp...  22.3 us
    pallas_call x1, Pallas kernels, on_device(): pl.pallas_call(deliver, out_shape=(jax.ShapeDtypeStruct((rows, width), jn...  0.84 us

profile of v6, /device:TPU:0, one launch (start us, length us, event | category | flops | bytes accessed | tf_op | source)
XLA Modules:
  0.0 23.7 jit_solution(1307934278639861575)
XLA Ops:
  0.6 22.3 %shard_map.59 = (f32[512,256]{1,0:T(8,128)S(1)}, f32[3,128]{1,0:T(4,128)S(1)}) custom-call(bf16[512,256]{1,0:T(8,128)(2,1)} %density_hbm.1, s32[2,4]{1,0:T(2,128)} %bitcast.3, s32[2,4]{1,0:T(2,128)} %bitcast.4, s32[4]{0:T(128)} %flag_hbm.1), custom_call_target="tpu_custom_call" | custom-call | tf_op jit(solution)/shard_map/pallas_call | solution.py:592
  22.9 0.8 %shard_map.60 = (f32[512,256]{1,0:T(8,128)}, f32[1,1]{1,0:T(1,128)}) custom-call(f32[512,256]{1,0:T(8,128)S(1)} %get-tuple-element.6.updated, f32[3,128]{1,0:T(4,128)S(1)} %get-tuple-element.7.lines), custom_call_target="tpu_custom_call" | custom-call | tf_op jit(solution)/shard_map/pallas_call | solution.py:633

commit v7 on v6

--- a/solution.py
+++ b/solution.py
@@ -26,7 +26,13 @@
     blocks = [[(b, q) for q in range(CHUNKS)] for b in range(n_row)]
     rightward = [sum(blocks[row::-1], []) for row in range(last)] + [[]]
     leftward = [[]] + [sum(blocks[row:], []) for row in range(1, n_row)]
-    leftward[1].append(leftward[1].pop(CHUNKS - 1))
+    for row in range(1, last):
+        for order, block, count in ((rightward[row], 1, 2), (leftward[row], last - 1, 1)):
+            for q in range(CHUNKS - count, CHUNKS):
+                order.remove((block, q))
+                order.append((block, q))
+    leftward[1].remove((1, CHUNKS - 1))
+    leftward[1].append((1, CHUNKS - 1))
     return rightward, leftward
 
 
@@ -358,7 +364,10 @@
 
         for z in range(last - 1, -1, -1):
             for col in range(n_col):
-                pl.when((z != r) | (col != c))(lambda: sum_copy(z, col, l).start())
+                if z:
+                    sum_copy(z, col, l).start()
+                else:
+                    pl.when(col != c)(lambda: sum_copy(z, col, l).start())
 
     everyone = [(z, col, layer) for z in range(n_row) for col in range(n_col)
                 for layer in range(n_layer)]
@@ -390,12 +399,15 @@
     def send_trace(row):
         trace_in[me] = trace_own[...]
         for z, col, layer in everyone:
-            pl.when((z != row) | (col != c) | (layer != l))(
-                lambda: trace_copy(z, col, layer).start())
+            if z != row:
+                trace_copy(z, col, layer).start()
+            else:
+                pl.when((col != c) | (layer != l))(
+                    lambda: trace_copy(z, col, layer).start())
 
     middle = (last - 1) * CHUNKS
-    pairs = {row: list(range(max(row + 1, 2 - row), n_row)) for row in range(n_row)}
-    pairs[1] += [0]
+    pairs = {row: [0] + list(range(row + 1, n_row)) for row in range(1, last)}
+    pairs.update({0: [last], last: []})
     asked = list(range(1, n_row))
 
     def ready_rows(count, distances):
@@ -446,15 +458,15 @@
         plane_arrive(d, 1)
     for k in range(CHUNKS, CHUNKS + 1):
         z_arrive(k)
+    for k in range(CHUNKS + 1, CHUNKS + 2):
+        z_arrive(k)
     def sides(chosen):
         side_wait(len(chosen) * (n_layer - 1), 2 if chosen is relayed else 1)
 
-    soon = ready_rows(CHUNKS + 1, direct)
+    soon = ready_rows(CHUNKS + 2, direct)
     in_soon = functools.reduce(jnp.logical_or, [r == row for row in soon], r < 0)
     pl.when(in_soon)(lambda: sides(direct))
     diagonals(soon)
-    for k in range(CHUNKS + 1, CHUNKS + 2):
-        z_arrive(k)
     for turn in range(2):
         for d in relayed:
             plane_arrive(d, turn)
@@ -494,7 +506,7 @@
             @pl.when(on_diagonal)
             def _():
                 add_trace(parts_of([(block, q)]), False)
-                if k == last * CHUNKS - 2:
+                if (block, q) == (last, CHUNKS - 1):
                     send_first()
         if k < last * CHUNKS - 1:
             add(terms(block, q * piece, piece))

time: 23.9 us -> 23.6 us (0.987); the launches traced: 23.7 us -> 23.1 us
  Pallas kernels: 23.1 us -> 22.5 us
    pallas_call x1, Pallas kernels: 22.3 us -> 21.6 us  [on_device(): pl.pallas_call(functools.partial(kernel, sizes), out_shape=(jax.ShapeDtyp...]
where the time goes in v7:
time: 23.6 us; the launch traced here: 23.1 us
  Pallas kernels  22.5 us (95%)
  between operations  0.64 us (3%)
    pallas_call x1, Pallas kernels, on_device(): pl.pallas_call(functools.partial(kernel, sizes), out_shape=(jax.ShapeDtyp...  21.6 us
    pallas_call x1, Pallas kernels, on_device(): pl.pallas_call(deliver, out_shape=(jax.ShapeDtypeStruct((rows, width), jn...  0.84 us

profile of v7, /device:TPU:0, one launch (start us, length us, event | category | flops | bytes accessed | tf_op | source)
XLA Modules:
  0.0 23.1 jit_solution(13709672918438800325)
XLA Ops:
  0.6 21.6 %shard_map.59 = (f32[512,256]{1,0:T(8,128)S(1)}, f32[3,128]{1,0:T(4,128)S(1)}) custom-call(bf16[512,256]{1,0:T(8,128)(2,1)} %density_hbm.1, s32[2,4]{1,0:T(2,128)} %bitcast.3, s32[2,4]{1,0:T(2,128)} %bitcast.4, s32[4]{0:T(128)} %flag_hbm.1), custom_call_target="tpu_custom_call" | custom-call | tf_op jit(solution)/shard_map/pallas_call | solution.py:604
  22.3 0.8 %shard_map.60 = (f32[512,256]{1,0:T(8,128)}, f32[1,1]{1,0:T(1,128)}) custom-call(f32[512,256]{1,0:T(8,128)S(1)} %get-tuple-element.6.updated, f32[3,128]{1,0:T(4,128)S(1)} %get-tuple-element.7.lines), custom_call_target="tpu_custom_call" | custom-call | tf_op jit(solution)/shard_map/pallas_call | solution.py:645

commit v8 on v7

--- a/solution.py
+++ b/solution.py
@@ -174,31 +174,36 @@
 
     on_diagonal = me // per == r
 
-    detour = bool(relayed) and n_layer <= len(bits)
-    by_way = functools.reduce(jnp.logical_or, [
-        (l == layer) & (c == bits[layer]) for layer in range(n_layer if detour else 0)],
-        c < 0)
-
-    def detour_copy(source, target, column, row, sem, recv):
+    detour = bool(relayed)
+    ways = [(c == d) & (l == n_layer - 1) for d in bits[:2]] if detour else []
+    by_way = functools.reduce(jnp.logical_or, ways, c < 0)
+
+    def part_of(h):
+        return pl.ds((CHUNKS - 1) * piece + h * (piece // 2), piece // 2)
+
+    def detour_copy(source, target, device, sem, recv):
         return pltpu.make_async_remote_copy(
             src_ref=source, dst_ref=target, send_sem=sem.at[0], recv_sem=recv,
-            device_id=(row, column, l), device_id_type=MESH,
+            device_id=device, device_id_type=MESH,
         )
 
     def detour_start():
-        for layer in range(n_layer):
-            pl.when((r == 1) & (c == 0) & (l == layer))(detour_copy(
-                row_panel.at[me, span(CHUNKS - 1)], aside, bits[layer], 1,
+        for h, d in enumerate(bits[:2]):
+            pl.when((r == 1) & (me == n_layer - 1))(detour_copy(
+                row_panel.at[me, part_of(h)], aside, (1, d, n_layer - 1),
                 left_send, aside_sems.at[0]).start)
 
     def detour_pass(row):
-        target, recv = ((aside, aside_sems.at[0]) if row else
-                        (col_panel.at[1, span(CHUNKS - 1)], z_recv.at[1, CHUNKS - 1]))
-
         @pl.when(by_way & (r == row))
         def _():
-            detour_copy(aside, aside, c, 0, aside_send, aside_sems.at[0]).wait_recv()
-            detour_copy(aside, target, c if row else 0, 0, aside_send, recv).start()
+            detour_copy(aside, aside, (0, c, l), aside_send, aside_sems.at[0]).wait_recv()
+            if row:
+                detour_copy(aside, aside, (0, c, l), aside_send, aside_sems.at[0]).start()
+
+        for h, way in enumerate(ways if row == 0 else []):
+            pl.when(way & (r == row))(detour_copy(
+                aside, col_panel.at[1, part_of(h)], (0, 0, n_layer - 1),
+                aside_send, z_recv.at[1, CHUNKS - 1]).start)
 
     def pass_on(copy, row, plan, first, arrived, stop=None, hold=None):
         while first < len(plan) and (stop is None or first < stop):
@@ -210,7 +215,7 @@
             else:
                 break
             if detour and copy is to_left and (row, block, q) == (1, 1, CHUNKS - 1):
-                pl.when(jnp.logical_not(on_diagonal) & (c > 0))(
+                pl.when(jnp.logical_not(on_diagonal) & (me != n_layer - 1))(
                     functools.partial(lambda f: f.start(), copy(block, q, source)))
             elif hold is None or first < hold:
                 copy(block, q, source).start()
@@ -538,7 +543,7 @@
 
     if detour:
         pl.when(by_way & (r < 2))(
-            detour_copy(aside, aside, c, 0, aside_send, aside_sems.at[0]).wait_send)
+            detour_copy(aside, aside, (0, c, l), aside_send, aside_sems.at[0]).wait_send)
     for row in range(n_row):
         @pl.when(r == row)
         def _():
@@ -630,7 +635,7 @@
             dma((2,)),
             pltpu.VMEM((n_layer, 3, blk), jnp.float32),
             pltpu.VMEM((3, blk), jnp.float32),
-            pltpu.VMEM((rows // CHUNKS, width), jnp.bfloat16),
+            pltpu.VMEM((rows // CHUNKS // 2, width), jnp.bfloat16),
             dma((1,)),
             dma((1,)),
             pltpu.SemaphoreType.REGULAR((4,)),

time: 23.6 us -> 23.2 us (0.983); the launches traced: 23.1 us -> 23 us
  no operation moved by 1% of the time
where the time goes in v8:
time: 23.2 us; the launch traced here: 23 us
  Pallas kernels  22.4 us (97%)
  between operations  0.64 us (3%)
    pallas_call x1, Pallas kernels, on_device(): pl.pallas_call(functools.partial(kernel, sizes), out_shape=(jax.ShapeDtyp...  21.6 us
    pallas_call x1, Pallas kernels, on_device(): pl.pallas_call(deliver, out_shape=(jax.ShapeDtypeStruct((rows, width), jn...  0.84 us

profile of v8, /device:TPU:0, one launch (start us, length us, event | category | flops | bytes accessed | tf_op | source)
XLA Modules:
  0.0 23.0 jit_solution(8966226275255198455)
XLA Ops:
  0.6 21.6 %shard_map.59 = (f32[512,256]{1,0:T(8,128)S(1)}, f32[3,128]{1,0:T(4,128)S(1)}) custom-call(bf16[512,256]{1,0:T(8,128)(2,1)} %density_hbm.1, s32[2,4]{1,0:T(2,128)} %bitcast.3, s32[2,4]{1,0:T(2,128)} %bitcast.4, s32[4]{0:T(128)} %flag_hbm.1), custom_call_target="tpu_custom_call" | custom-call | tf_op jit(solution)/shard_map/pallas_call | solution.py:609
  22.2 0.8 %shard_map.60 = (f32[512,256]{1,0:T(8,128)}, f32[1,1]{1,0:T(1,128)}) custom-call(f32[512,256]{1,0:T(8,128)S(1)} %get-tuple-element.6.updated, f32[3,128]{1,0:T(4,128)S(1)} %get-tuple-element.7.lines), custom_call_target="tpu_custom_call" | custom-call | tf_op jit(solution)/shard_map/pallas_call | solution.py:650

commit v9 on v8

--- a/solution.py
+++ b/solution.py
@@ -40,8 +40,8 @@
     sizes, density_hbm, block_hbm, keep_hbm, flag_hbm, updated, lines,
     density, block_mask, keep_mask, branch_flag,
     row_panel, col_panel, trace_own, trace_in, local_sem,
-    plane_send, plane_recv, side_send, side_recv, right_send, left_send, z_recv,
-    trace_send, trace_recv, trace_swap, trace_sum, aside, aside_send, aside_sems, ready,
+    plane_send, plane_recv, side_recv, z_send, z_recv,
+    trace_send, trace_recv, trace_swap, trace_sum, aside, aplane_send, aside_sems, ready,
 ):
     n_row, n_col, n_layer = sizes
     rows, width = density.shape
@@ -77,15 +77,16 @@
     def span(q):
         return pl.ds(q * piece, piece)
 
-    loads = [
-        pltpu.make_async_copy(source, target, local_sem.at[i])
-        for i, (source, target) in enumerate(
-            [(block_hbm, block_mask)]
-            + [(density_hbm.at[span(q)], density.at[span(q)]) for q in range(CHUNKS)]
-            + [(keep_hbm, keep_mask), (flag_hbm, branch_flag)])
-    ]
-    for load in loads:
-        load.start()
+    def load(n, source, target):
+        return pltpu.make_async_copy(source, target, local_sem.at[n])
+
+    rest = pl.ds(piece, rows - piece)
+    load_first = load(0, density_hbm.at[span(0)], density.at[span(0)])
+    load_mask = load(1, block_hbm, block_mask)
+    load_rest = load(2, density_hbm.at[rest], density.at[rest])
+    load_keep, load_flag = load(0, keep_hbm, keep_mask), load(1, flag_hbm, branch_flag)
+    for first in (load_first, load_mask, load_rest):
+        first.start()
 
     barrier = pltpu.get_barrier_semaphore()
 
@@ -105,27 +106,31 @@
     for p, q, met, to in plane_peers:
         pl.when((p * n_layer + q < me) & met)(functools.partial(answer, to, (r, p, q)))
     def mask(q):
-        loads[1 + q].wait()
+        if q == 1:
+            load_rest.wait()
         for i in range(q * piece // blk, (q + 1) * piece // blk):
             for k in range(width // blk):
                 at = (pl.ds(i * blk, blk), pl.ds(k * blk, blk))
                 kept = jnp.full((blk, blk), block_mask[k, i].astype(jnp.float32))
                 row_panel[(me,) + at] = density[at] * kept.astype(jnp.bfloat16)
 
-    loads[0].wait()
-
-    def z_copy(block, q, source, target, sem):
+    load_mask.wait()
+    load_first.wait()
+    load_keep.start()
+    load_flag.start()
+
+    def z_copy(block, q, source, target, sem, recv):
         return pltpu.make_async_remote_copy(
             src_ref=source, dst_ref=col_panel.at[block, span(q)],
-            send_sem=sem.at[0], recv_sem=z_recv.at[block, q],
+            send_sem=sem.at[0], recv_sem=z_recv.at[recv, q],
             device_id=(target, c, l), device_id_type=MESH,
         )
 
     def to_right(block, q, source):
-        return z_copy(block, q, source, right, right_send)
+        return z_copy(block, q, source, right, z_send, block)
 
     def to_left(block, q, source):
-        return z_copy(block, q, source, left, left_send)
+        return z_copy(block, q, source, left, z_send, block - 1)
 
     def half_copy(slot, h, sem, recv, target):
         half = pl.ds(h * (rows // 2), rows // 2)
@@ -139,13 +144,13 @@
 
     def side_copies(slot, h, group):
         for other in layer_peers:
-            half_copy(slot, h, side_send, side_recv.at[group], (r, c, other)).start()
+            half_copy(slot, h, plane_send, side_recv.at[group], (r, c, other)).start()
 
     def side_wait(count, group):
         blocks = row_panel.at[pl.ds(0, count)]
         if count:
             pltpu.make_async_remote_copy(
-                src_ref=blocks, dst_ref=blocks, send_sem=side_send.at[0],
+                src_ref=blocks, dst_ref=blocks, send_sem=plane_send.at[0],
                 recv_sem=side_recv.at[group], device_id=(r, c, l), device_id_type=MESH,
             ).wait_recv()
 
@@ -191,19 +196,19 @@
         for h, d in enumerate(bits[:2]):
             pl.when((r == 1) & (me == n_layer - 1))(detour_copy(
                 row_panel.at[me, part_of(h)], aside, (1, d, n_layer - 1),
-                left_send, aside_sems.at[0]).start)
+                z_send, aside_sems.at[0]).start)
 
     def detour_pass(row):
         @pl.when(by_way & (r == row))
         def _():
-            detour_copy(aside, aside, (0, c, l), aside_send, aside_sems.at[0]).wait_recv()
+            detour_copy(aside, aside, (0, c, l), aplane_send, aside_sems.at[0]).wait_recv()
             if row:
-                detour_copy(aside, aside, (0, c, l), aside_send, aside_sems.at[0]).start()
+                detour_copy(aside, aside, (0, c, l), aplane_send, aside_sems.at[0]).start()
 
         for h, way in enumerate(ways if row == 0 else []):
             pl.when(way & (r == row))(detour_copy(
                 aside, col_panel.at[1, part_of(h)], (0, 0, n_layer - 1),
-                aside_send, z_recv.at[1, CHUNKS - 1]).start)
+                aplane_send, z_recv.at[0, CHUNKS - 1]).start)
 
     def pass_on(copy, row, plan, first, arrived, stop=None, hold=None):
         while first < len(plan) and (stop is None or first < stop):
@@ -234,8 +239,6 @@
             def _():
                 sent_left[row] = pass_on(
                     to_left, row, leftward[row], sent_left[row], (), q + 1)
-    for load in loads[1 + CHUNKS:]:
-        load.wait()
     plane_start(lambda peer: peer < c)
     pl.when(has_right)(lambda: pl.semaphore_wait(ready.at[0], 1))
     for row in range(last):
@@ -442,6 +445,8 @@
             hold_left.pop(row, None)
             hold_right.pop(row, None)
 
+    load_keep.wait()
+    load_flag.wait()
     pl.when(far_above > 0)(lambda: pl.semaphore_wait(ready.at[3], far_above))
     @pl.when(r == last)
     def _():
@@ -543,20 +548,14 @@
 
     if detour:
         pl.when(by_way & (r < 2))(
-            detour_copy(aside, aside, (0, c, l), aside_send, aside_sems.at[0]).wait_send)
+            detour_copy(aside, aside, (0, c, l), aplane_send, aside_sems.at[0]).wait_send)
     for row in range(n_row):
-        @pl.when(r == row)
-        def _():
-            for copy, plan, sem in (
-                    (to_left, leftward[row], left_send),
-                    (to_right, rightward[row], right_send)):
-                if plan:
-                    blocks = pl.ds(0, len(plan) // CHUNKS)
-                    pltpu.make_async_remote_copy(
-                        src_ref=col_panel.at[blocks], dst_ref=col_panel.at[blocks],
-                        send_sem=sem.at[0], recv_sem=z_recv.at[0, 0],
-                        device_id=(left, c, l), device_id_type=MESH,
-                    ).wait_send()
+        blocks = pl.ds(0, (len(leftward[row]) + len(rightward[row])) // CHUNKS)
+        pl.when(r == row)(pltpu.make_async_remote_copy(
+            src_ref=row_panel.at[blocks], dst_ref=row_panel.at[blocks],
+            send_sem=z_send.at[0], recv_sem=z_recv.at[0, 0],
+            device_id=(left, c, l), device_id_type=MESH,
+        ).wait_send)
 
     def sent_slots(count, ref, sem):
         pltpu.make_async_remote_copy(
@@ -565,8 +564,7 @@
             device_id=(r, c, l), device_id_type=MESH,
         ).wait_send()
 
-    sent_slots(n_col - 1, row_panel, plane_send)
-    sent_slots((n_layer - 1) * n_col, row_panel, side_send)
+    sent_slots(n_layer * n_col - 1, row_panel, plane_send)
 
     def heard(count):
         pltpu.make_async_remote_copy(
@@ -623,14 +621,12 @@
             pltpu.VMEM((n_row, rows, width), jnp.bfloat16),
             pltpu.VMEM((3, blk), jnp.float32),
             pltpu.VMEM((n_row * slots, 3, blk), jnp.float32),
-            dma((CHUNKS + 3,)),
+            dma((3,)),
             dma((1,)),
             dma((max(n_col - 1, 1), 2)),
-            dma((1,)),
             dma((3,)),
             dma((1,)),
-            dma((1,)),
-            dma((n_row, CHUNKS)),
+            dma((n_row - 1, CHUNKS)),
             dma((1,)),
             dma((2,)),
             pltpu.VMEM((n_layer, 3, blk), jnp.float32),

time: 23.2 us -> 23.1 us (level)
  no operation moved by 1% of the time
where the time goes in v9:
time: 23.1 us; the launch traced here: 23 us
  Pallas kernels  22.3 us (97%)
  between operations  0.64 us (3%)
    pallas_call x1, Pallas kernels, on_device(): pl.pallas_call(functools.partial(kernel, sizes), out_shape=(jax.ShapeDtyp...  21.5 us
    pallas_call x1, Pallas kernels, on_device(): pl.pallas_call(deliver, out_shape=(jax.ShapeDtypeStruct((rows, width), jn...  0.84 us

profile of v9, /device:TPU:0, one launch (start us, length us, event | category | flops | bytes accessed | tf_op | source)
XLA Modules:
  0.0 23.0 jit_solution(62104313405064410)
XLA Ops:
  0.6 21.5 %shard_map.59 = (f32[512,256]{1,0:T(8,128)S(1)}, f32[3,128]{1,0:T(4,128)S(1)}) custom-call(bf16[512,256]{1,0:T(8,128)(2,1)} %density_hbm.1, s32[2,4]{1,0:T(2,128)} %bitcast.3, s32[2,4]{1,0:T(2,128)} %bitcast.4, s32[4]{0:T(128)} %flag_hbm.1), custom_call_target="tpu_custom_call" | custom-call | tf_op jit(solution)/shard_map/pallas_call | solution.py:607
  22.1 0.8 %shard_map.60 = (f32[512,256]{1,0:T(8,128)}, f32[1,1]{1,0:T(1,128)}) custom-call(f32[512,256]{1,0:T(8,128)S(1)} %get-tuple-element.6.updated, f32[3,128]{1,0:T(4,128)S(1)} %get-tuple-element.7.lines), custom_call_target="tpu_custom_call" | custom-call | tf_op jit(solution)/shard_map/pallas_call | solution.py:646

commit v10 on v9

--- a/solution.py
+++ b/solution.py
@@ -231,7 +231,7 @@
         return first
 
     sent_left, sent_right = [0] * n_row, [0] * n_row
-    hold_left, hold_right = {1: last * CHUNKS - 2}, {last - 1: 2 * CHUNKS - 1}
+    hold_left, hold_right = {1: last * CHUNKS - 2}, {last - 1: 2 * CHUNKS}
     for q in range(CHUNKS):
         mask(q)
         for row in range(1, n_row) if q < AHEAD else []:
@@ -590,9 +590,14 @@
             functools.partial(sent_slots, count, trace_in, trace_send))
 
 
-def deliver(updated, lines, out, trace):
-    out[...] = updated[...]
-    trace[0, 0] = jnp.sum(lines[0:1, :] + lines[1:2, :] * lines[2:3, :])
+def deliver(updated, lines, out, trace, total, sems):
+    whole = pltpu.make_async_copy(updated, out, sems.at[0])
+    whole.start()
+    total[...] = jnp.sum(lines[0:1, :] + lines[1:2, :] * lines[2:3, :], keepdims=True)
+    single = pltpu.make_async_copy(total, trace, sems.at[1])
+    single.start()
+    whole.wait()
+    single.wait()
 
 
 def on_device(sizes, density, block_mask, keep_mask, branch_flag):
@@ -601,7 +606,7 @@
     blk = rows // block_mask.shape[0]
     dma = pltpu.SemaphoreType.DMA
     slots = n_col * n_layer
-    vmem, smem = pl.BlockSpec(memory_space=pltpu.VMEM), pl.BlockSpec(memory_space=pltpu.SMEM)
+    vmem = pl.BlockSpec(memory_space=pltpu.VMEM)
     hbm = pl.BlockSpec(memory_space=pltpu.HBM)
     panel_bytes = 2 * rows * width * (slots + n_row + 1)
     updated, lines = pl.pallas_call(
@@ -650,7 +655,8 @@
             jax.ShapeDtypeStruct((1, 1), jnp.float32),
         ),
         in_specs=[vmem, vmem],
-        out_specs=(vmem, smem),
+        out_specs=(hbm, hbm),
+        scratch_shapes=[pltpu.VMEM((1, 1), jnp.float32), dma((2,))],
         compiler_params=pltpu.CompilerParams(
             vmem_limit_bytes=8 * rows * width + (4 << 20)),
     )(updated, lines)

time: 23.1 us -> 23.1 us (level)
  no operation moved by 1% of the time
where the time goes in v10:
time: 23.1 us; the launch traced here: 22.9 us
  Pallas kernels  22.3 us (97%)
  between operations  0.64 us (3%)
    pallas_call x1, Pallas kernels, on_device(): pl.pallas_call(functools.partial(kernel, sizes), out_shape=(jax.ShapeDtyp...  21.5 us
    pallas_call x1, Pallas kernels, on_device(): pl.pallas_call(deliver, out_shape=(jax.ShapeDtypeStruct((rows, width), jn...  0.81 us

profile of v10, /device:TPU:0, one launch (start us, length us, event | category | flops | bytes accessed | tf_op | source)
XLA Modules:
  0.0 22.9 jit_solution(14451669718948581898)
XLA Ops:
  0.6 21.5 %shard_map.59 = (f32[512,256]{1,0:T(8,128)S(1)}, f32[3,128]{1,0:T(4,128)S(1)}) custom-call(bf16[512,256]{1,0:T(8,128)(2,1)} %density_hbm.1, s32[2,4]{1,0:T(2,128)} %bitcast.3, s32[2,4]{1,0:T(2,128)} %bitcast.4, s32[4]{0:T(128)} %flag_hbm.1), custom_call_target="tpu_custom_call" | custom-call | tf_op jit(solution)/shard_map/pallas_call | solution.py:612
  22.1 0.8 %shard_map.60 = (f32[512,256]{1,0:T(8,128)}, f32[1,1]{1,0:T(1,128)}) custom-call(f32[512,256]{1,0:T(8,128)S(1)} %get-tuple-element.6.updated, f32[3,128]{1,0:T(4,128)S(1)} %get-tuple-element.7.lines), custom_call_target="tpu_custom_call" | custom-call | tf_op jit(solution)/shard_map/pallas_call | solution.py:651

commit v11 on v9

--- a/solution.py
+++ b/solution.py
@@ -231,7 +231,7 @@
         return first
 
     sent_left, sent_right = [0] * n_row, [0] * n_row
-    hold_left, hold_right = {1: last * CHUNKS - 2}, {last - 1: 2 * CHUNKS - 1}
+    hold_left, hold_right = {1: last * CHUNKS - 2}, {last - 1: 2 * CHUNKS}
     for q in range(CHUNKS):
         mask(q)
         for row in range(1, n_row) if q < AHEAD else []:

time: 23.1 us -> 23.1 us (level)
  no operation moved by 1% of the time
where the time goes in v11:
time: 23.1 us; the launch traced here: 23 us
  Pallas kernels  22.3 us (97%)
  between operations  0.64 us (3%)
    pallas_call x1, Pallas kernels, on_device(): pl.pallas_call(functools.partial(kernel, sizes), out_shape=(jax.ShapeDtyp...  21.5 us
    pallas_call x1, Pallas kernels, on_device(): pl.pallas_call(deliver, out_shape=(jax.ShapeDtypeStruct((rows, width), jn...  0.84 us

profile of v11, /device:TPU:0, one launch (start us, length us, event | category | flops | bytes accessed | tf_op | source)
XLA Modules:
  0.0 23.0 jit_solution(16107740696920837010)
XLA Ops:
  0.6 21.5 %shard_map.59 = (f32[512,256]{1,0:T(8,128)S(1)}, f32[3,128]{1,0:T(4,128)S(1)}) custom-call(bf16[512,256]{1,0:T(8,128)(2,1)} %density_hbm.1, s32[2,4]{1,0:T(2,128)} %bitcast.3, s32[2,4]{1,0:T(2,128)} %bitcast.4, s32[4]{0:T(128)} %flag_hbm.1), custom_call_target="tpu_custom_call" | custom-call | tf_op jit(solution)/shard_map/pallas_call | solution.py:607
  22.1 0.8 %shard_map.60 = (f32[512,256]{1,0:T(8,128)}, f32[1,1]{1,0:T(1,128)}) custom-call(f32[512,256]{1,0:T(8,128)S(1)} %get-tuple-element.6.updated, f32[3,128]{1,0:T(4,128)S(1)} %get-tuple-element.7.lines), custom_call_target="tpu_custom_call" | custom-call | tf_op jit(solution)/shard_map/pallas_call | solution.py:646
